TPU v7x, 32 devices: a whole 2x2x4 slice. The times are simulated.
32 devices in a mesh: scene: 2 (over x), mrow: 8 (over z, y), mcol: 2 (over core).
Axes of the slice: x: 2, y: 2, z: 4, core: 2. Of those that a mesh axis runs over, the one named last changes fastest.
Arguments:
- pan_blocks: bfloat16 [2048, 128, 128], P(('scene', 'mrow', 'mcol')), parts along dimension 0, may hold values from -6 to 6
- ms_blocks: bfloat16 [2048, 32, 256], P(('scene', 'mrow', 'mcol')), parts along dimension 0, may hold values from -6 to 6
- send_list: int32 [3, 2048], P(None, ('scene', 'mrow', 'mcol')), parts along dimension 1, may hold values from 0 to 127, as said below
- tile_list: int32 [3, 4096], P(None, ('scene', 'mrow', 'mcol')), parts along dimension 1, may hold values from 0 to 9, as said below
- row_grid: float32 [48], P(('scene', 'mrow')), parts along dimension 0, may hold values from -32 to 288
- col_grid: float32 [16, 16], P(('scene', 'mrow'), 'mcol'), parts along dimension 0, may hold values from -32 to 1312
- band_mix: float32 [8, 8], replicated, may hold values from -1.5 to 1.5
- band_gain: float32 [8], replicated, may hold values from 0.4 to 1.2
- synth_weight: float32 [8], replicated, may hold values from 0.05 to 0.3
Outputs:
- sharpened: bfloat16 [8, 2048, 1024], P(None, ('scene', 'mrow'), 'mcol'), parts along dimension 1
There are 2 independent parts, one for each index of `scene`. A program takes and returns all parts, laid end to end along the dimension named above; an argument that names none is the same for every part. Nothing has to cross between parts.
Inputs may be any that keep to these rules, and one draw needn't show every extreme that they name: `send_list`: row 0 gives each source block of a device a distinct send slot; slot p goes to map-row owner p // 16 in the device's own map column, so one device sends at most 16 blocks to one tile; in every draw one tile of each map column receives 16 blocks from every device of that column, and every device fills 16 slots of it. Row 1 is a cell row below 2; row 2 a cell column between mcol * 5 and mcol * 5 + 4. `tile_list`: row 0 is 1 exactly in the receive slots that send_list fills and 0 elsewhere; rows 1 and 2 repeat the cell row and column of the block sent there, and are 0 in empty slots.
All inputs are finite; a program needn't handle non-finite values.
Results may differ from a plain program's by a relative error of at most 0.0073.
Values may be sent and summed in bfloat16 or wider, within the bound.
A program may use at most 128 MiB of HBM per device.

v0:
```python
import functools

import jax
import jax.numpy as jnp
from jax import lax
from jax.experimental import pallas as pl
from jax.experimental.pallas import tpu as pltpu
from jax.sharding import PartitionSpec as P

GRID = 64
TR = 128
TC = 512
KR = 2
KC = 5
MESH = pl.DeviceIdType.MESH
F32 = jnp.float32
BF16 = jnp.bfloat16


def cubic_weight(offset):
    outer = jnp.maximum(2.0 - jnp.abs(offset), 0.0)
    shifted = outer - 1.0
    inner = jnp.maximum(shifted, 0.0)
    return outer * outer * (0.5 * shifted) + inner * inner * (1.0 - 2.0 * inner)


def iota(shape, dim):
    return lax.broadcasted_iota(jnp.int32, shape, dim)


def cell_sums(
    capacity,
    send_ref,
    pan_hbm,
    ms_hbm,
    row_ref,
    col_ref,
    pan_out,
    ms_out,
    nodes_out,
    first_block,
    next_block,
    pan_ref,
    ms_ref,
    load_sem,
):
    tile = pl.program_id(0)
    own_blocks, block_size, _ = pan_ref.shape
    _, coarse_size, coarse_width = ms_ref.shape
    first_col = lax.axis_index("mcol") * KC

    @pl.when(tile == 0)
    def _():
        pan_load = pltpu.make_async_copy(pan_hbm, pan_ref, load_sem.at[0])
        ms_load = pltpu.make_async_copy(ms_hbm, ms_ref, load_sem.at[1])
        pan_load.start()
        ms_load.start()
        nodes_out[...] = jnp.zeros_like(nodes_out)
        nodes_out[0:1, 0 : row_ref.shape[1]] = row_ref[...]
        nodes_out[1:2, 0 : col_ref.shape[1]] = col_ref[...]

        def clear(k, carry):
            for r in range(KR * KC):
                first_block[k * (KR * KC) + r] = -1
            return carry

        lax.fori_loop(0, first_block.shape[0] // (KR * KC), clear, 0)

        def enter(block, carry):
            cell = (send_ref[0, block] // capacity * KR + send_ref[1, block]) * KC
            cell = cell + send_ref[2, block] - first_col
            next_block[block] = first_block[cell]
            first_block[cell] = block
            return carry

        lax.fori_loop(0, own_blocks, enter, 0, unroll=4)
        pan_load.wait()
        ms_load.wait()

    for row in range(KR):
        for col in range(KC):

            def add(carry):
                block, pan, ms = carry
                pan = pan + pan_ref[block].astype(F32)
                ms = ms + ms_ref[block].astype(F32)
                return next_block[block], pan, ms

            start = (
                first_block[(tile * KR + row) * KC + col],
                jnp.zeros((block_size, block_size), F32),
                jnp.zeros((coarse_size, coarse_width), F32),
            )
            _, pan, ms = lax.while_loop(lambda carry: carry[0] >= 0, add, start)
            rows = slice(row * block_size, (row + 1) * block_size)
            pan_out[0, rows, col * block_size : (col + 1) * block_size] = pan.astype(BF16)
            rows = slice(row * coarse_size, (row + 1) * coarse_size)
            ms_out[0, rows, col * coarse_width : (col + 1) * coarse_width] = ms.astype(BF16)


def row_coord(nodes, position, offset):
    first = position < GRID
    a = jnp.where(first, nodes[0:1, 0:1], nodes[0:1, 1:2])
    b = jnp.where(first, nodes[0:1, 1:2], nodes[0:1, 2:3])
    within = (jnp.where(first, position, position - GRID).astype(F32) + offset) / GRID
    return a + (b - a) * within


def col_coord(nodes, after, is_last, count, position, offset):
    segment = position // GRID
    coord = jnp.zeros(position.shape, F32)
    for s in range(count):
        left, shift = nodes[1:2, s : s + 1], s * GRID
        if s + 1 < count:
            right = nodes[1:2, s + 1 : s + 2]
        else:
            right = jnp.where(is_last, left, after)
            left = jnp.where(is_last, nodes[1:2, s - 1 : s], left)
            shift = jnp.where(is_last, shift - GRID, shift)
        within = ((position - shift).astype(F32) + offset) / GRID
        coord = jnp.where(segment == s, left + (right - left) * within, coord)
    return coord


def mapping(
    col_nodes,
    nodes_ref,
    pan_hbm,
    ms_hbm,
    mix_ref,
    gain_ref,
    synth_ref,
    mixed_hbm,
    pan_map,
    pan_ref,
    ms_ref,
    nodes_all,
    ms_pair_send,
    ms_pair_recv,
    ms_owner_send,
    ms_owner_recv,
    pan_pair_send,
    pan_pair_recv,
    pan_owner_send,
    pan_owner_recv,
    ms_total,
    col_weight,
    ms_col_weight,
    window,
    beside,
    up_cols,
    up_rows,
    mixed,
    load_sem,
    nodes_ss,
    nodes_rs,
    ms_pair_ss,
    ms_pair_rs,
    ms_owner_ss,
    ms_owner_rs,
    pan_pair_ss,
    pan_pair_rs,
    pan_owner_ss,
    pan_owner_rs,
    halo_ss,
    halo_rs,
):
    n = lax.axis_size("mrow")
    pairs = n // 2
    scene = lax.axis_index("scene")
    m = lax.axis_index("mrow")
    c = lax.axis_index("mcol")
    z, y = m // 2, m % 2
    twin = z * 2 + (1 - y)
    other = 1 - c
    cols = pan_ref.shape[2]
    pan_rows = pan_ref.shape[1]
    ms_rows = ms_ref.shape[1]
    bands = mixed.shape[0]
    coarse_rows = TR // 4
    coarse_cols = TC // 4
    half = coarse_rows // 2
    mid = half + coarse_rows
    coarse_size = ms_rows // KR
    is_last = c == lax.axis_size("mcol") - 1

    def at(row, col):
        return (scene, row, col)

    def line_of(k):
        return lax.rem(z + 1 + lax.rem(pairs // 2 - 1 + k, pairs - 1), pairs)

    barrier = pltpu.get_barrier_semaphore()

    def greet(k, carry):
        row = lax.rem(m + k, n)
        pl.semaphore_signal(barrier, inc=1, device_id=at(row, c), device_id_type=MESH)
        pl.semaphore_signal(barrier, inc=1, device_id=at(row, other), device_id_type=MESH)
        return carry

    pl.semaphore_signal(barrier, inc=1, device_id=at(m, other), device_id_type=MESH)
    lax.fori_loop(1, n, greet, 0)
    ms_load = pltpu.make_async_copy(ms_hbm, ms_ref, load_sem.at[0])
    pan_load = pltpu.make_async_copy(pan_hbm, pan_ref, load_sem.at[1])
    ms_load.start()
    pan_load.start()

    tap = iota((TR, 2 * coarse_rows), 1) - (half - 2)
    spot = (iota((TR, 2 * coarse_rows), 0).astype(F32) - 1.5) * 0.25 + 2.0
    up_rows[...] = cubic_weight(spot - tap.astype(F32)).astype(BF16)
    ms_col_weight[...] = jnp.zeros_like(ms_col_weight)
    pl.semaphore_wait(barrier, 2 * n - 1)

    def nodes_copy(slot_row, slot_col, row, col):
        return pltpu.make_async_remote_copy(
            src_ref=nodes_ref,
            dst_ref=nodes_all.at[slot_col, slot_row],
            send_sem=nodes_ss.at[col, row],
            recv_sem=nodes_rs.at[slot_col, slot_row],
            device_id=at(row, col),
            device_id_type=MESH,
        )

    def send_nodes(k, carry):
        row = lax.rem(m + k, n)
        nodes_copy(m, c, row, c).start()
        nodes_copy(m, c, row, other).start()
        return carry

    lax.fori_loop(1, n, send_nodes, 0)
    nodes_copy(m, c, m, other).start()
    nodes_all[c, m] = nodes_ref[...]

    spot = (iota((coarse_cols, TC), 1).astype(F32) - 1.5) * 0.25 + 2.0
    tap = iota((coarse_cols, TC), 0) + 2
    up_cols[0] = cubic_weight(spot - tap.astype(F32)).astype(BF16)
    tap = tap + jnp.where(c == 0, coarse_cols, -coarse_cols)
    up_cols[1] = cubic_weight(spot - tap.astype(F32)).astype(BF16)
    ms_load.wait()

    def wait_nodes(k, carry):
        row = lax.rem(m + k, n)
        nodes_copy(row, c, row, c).wait()
        nodes_copy(row, other, row, other).wait()
        return carry

    lax.fori_loop(1, n, wait_nodes, 0)
    nodes_copy(m, other, m, other).wait()

    sides = (slice(0, coarse_rows), slice(coarse_rows, 2 * coarse_rows))

    def ms_part(tile):
        nodes = nodes_all[c, tile]
        shape = (coarse_rows, ms_rows)
        spots = (row_coord(nodes, 4 * iota(shape, 0) + 1, 0.5) - 1.5) * 0.25
        weight = cubic_weight(spots - iota(shape, 1).astype(F32)).astype(BF16)
        left = jnp.dot(weight, ms_ref[tile, :, 0:cols], preferred_element_type=F32)
        right = jnp.dot(weight, ms_ref[tile, :, cols : 2 * cols], preferred_element_type=F32)
        return left, right

    def pan_part(tile):
        nodes = nodes_all[c, tile]
        after = nodes_all[1, tile][1:2, 0:1]
        x_pan = col_coord(nodes, after, is_last, col_nodes, iota((1, TC), 1), 0.0)
        size = cols // KC
        for k in range(KC):
            pixel = (c * KC + k) * size + iota((size, TC), 0)
            col_weight[k * size : (k + 1) * size, :] = cubic_weight(
                x_pan - pixel.astype(F32)
            ).astype(BF16)
        shape = (TR, pan_rows)
        weight = cubic_weight(
            row_coord(nodes, iota(shape, 0), 0.0) - iota(shape, 1).astype(F32)
        ).astype(BF16)
        rows = jnp.dot(weight, pan_ref[tile], preferred_element_type=F32)
        return jnp.dot(rows.astype(BF16), col_weight[...], preferred_element_type=F32)

    def pair_copy(send, recv, ss, rs, k):
        return pltpu.make_async_remote_copy(
            src_ref=send.at[k],
            dst_ref=recv.at[k],
            send_sem=ss.at[k],
            recv_sem=rs.at[k],
            device_id=at(twin, c),
            device_id_type=MESH,
        )

    def owner_copy(send, recv, ss, rs, k, line, slot):
        return pltpu.make_async_remote_copy(
            src_ref=send.at[k],
            dst_ref=recv.at[slot],
            send_sem=ss.at[k],
            recv_sem=rs.at[slot],
            device_id=at(line * 2 + y, c),
            device_id_type=MESH,
        )

    ms_pair = functools.partial(pair_copy, ms_pair_send, ms_pair_recv, ms_pair_ss, ms_pair_rs)
    pan_pair = functools.partial(pair_copy, pan_pair_send, pan_pair_recv, pan_pair_ss, pan_pair_rs)
    ms_owner = functools.partial(
        owner_copy, ms_owner_send, ms_owner_recv, ms_owner_ss, ms_owner_rs
    )
    pan_owner = functools.partial(
        owner_copy, pan_owner_send, pan_owner_recv, pan_owner_ss, pan_owner_rs
    )

    def ms_to_twin(k, tile):
        for side, value in zip(sides, ms_part(tile)):
            ms_pair_send[k, side, :] = value.astype(BF16)
        ms_pair(k).start()

    def pan_to_twin(k, tile):
        pan_pair_send[k] = pan_part(tile).astype(BF16)
        pan_pair(k).start()

    def each_line(first, last, step):
        def body(k, carry):
            step(k, line_of(k))
            return carry

        lax.fori_loop(first, last, body, 0)

    each_line(0, pairs - 1, lambda k, line: ms_to_twin(k, line * 2 + 1 - y))
    ms_to_twin(pairs - 1, twin)
    pan_load.wait()
    each_line(0, pairs - 1, lambda k, line: pan_to_twin(k, line * 2 + 1 - y))
    pan_to_twin(pairs - 1, twin)

    def ms_to_owner(k, line):
        values = ms_part(line * 2 + y)
        ms_pair(k).wait()
        for side, value in zip(sides, values):
            ms_owner_send[k, side, :] = (value + ms_pair_recv[k, side, :].astype(F32)).astype(BF16)
        ms_owner(k, line, z).start()

    each_line(0, pairs - 1, ms_to_owner)
    values = ms_part(m)
    ms_pair(pairs - 1).wait()
    for side, value in zip(sides, values):
        ms_total[side, :] = value + ms_pair_recv[pairs - 1, side, :].astype(F32)

    x_ms = col_coord(
        nodes_ref[...],
        nodes_all[1, m][1:2, 0:1],
        is_last,
        col_nodes,
        4 * iota((1, coarse_cols), 1) + 1,
        0.5,
    )
    x_ms = (x_ms - 1.5) * 0.25
    for k in range(KC):
        pixel = (c * KC + k) * coarse_size + iota((coarse_size, coarse_cols), 0)
        weight = cubic_weight(x_ms - pixel.astype(F32)).astype(BF16)
        for b in range(bands):
            row = (k * bands + b) * coarse_size
            ms_col_weight[row : row + coarse_size, b * coarse_cols : (b + 1) * coarse_cols] = weight

    def pan_to_owner(k, line):
        value = pan_part(line * 2 + y)
        pan_pair(k).wait()
        pan_owner_send[k] = (value + pan_pair_recv[k].astype(F32)).astype(BF16)
        pan_owner(k, line, z).start()

    each_line(0, pairs - 2, pan_to_owner)

    def ms_from_line(k, line):
        ms_owner(k, line, line).wait()
        ms_total[...] += ms_owner_recv[line].astype(F32)

    each_line(0, pairs - 1, ms_from_line)
    left, right = [ms_total[side, :].astype(BF16) for side in sides]
    ms_map = jnp.dot(left, ms_col_weight[0:cols, :], preferred_element_type=F32)
    ms_map = ms_map + jnp.dot(
        right, ms_col_weight[cols : 2 * cols, :], preferred_element_type=F32
    )
    values = [ms_map[:, b * coarse_cols : (b + 1) * coarse_cols] for b in range(bands)]
    synthetic = sum(synth_ref[b] * values[b] for b in range(bands))
    for b in range(bands):
        result = values[b] - gain_ref[b] * synthetic
        for k in range(bands):
            result = result + mix_ref[b, k] * values[k]
        window[half:mid, b * coarse_cols : (b + 1) * coarse_cols] = result.astype(BF16)

    has_above, has_below = m > 0, m < n - 1

    def halo_copy(k, src, rows, dst, start, row, col):
        return pltpu.make_async_remote_copy(
            src_ref=window.at[pl.ds(src, rows)],
            dst_ref=dst.at[pl.ds(start, rows)],
            send_sem=halo_ss.at[k],
            recv_sem=halo_rs.at[k],
            device_id=at(row, col),
            device_id_type=MESH,
        )

    across_copy = halo_copy(0, half, coarse_rows, beside, half, m, other)
    up_copies = [
        halo_copy(1, half, half, window, mid, m - 1, c),
        halo_copy(2, half, half, beside, mid, m - 1, other),
    ]
    down_copies = [
        halo_copy(3, coarse_rows, half, window, 0, m + 1, c),
        halo_copy(4, coarse_rows, half, beside, 0, m + 1, other),
    ]
    across_copy.start()

    @pl.when(has_above)
    def _():
        for copy in up_copies:
            copy.start()

    @pl.when(has_below)
    def _():
        for copy in down_copies:
            copy.start()

    pan_to_owner(pairs - 2, line_of(pairs - 2))
    pan_map[...] = pan_part(m)
    across_copy.wait()

    @pl.when(has_above)
    def _():
        for copy in up_copies:
            copy.wait_send()
        for copy in down_copies:
            copy.wait_recv()

    @pl.when(has_below)
    def _():
        for copy in down_copies:
            copy.wait_send()
        for copy in up_copies:
            copy.wait_recv()

    edge = jnp.zeros((half, window.shape[1]), BF16)

    @pl.when(jnp.logical_not(has_above))
    def _():
        window[0:half, :] = edge
        beside[0:half, :] = edge

    @pl.when(jnp.logical_not(has_below))
    def _():
        window[mid : mid + half, :] = edge
        beside[mid : mid + half, :] = edge

    for b in range(bands):
        lanes = slice(b * coarse_cols, (b + 1) * coarse_cols)
        across = jnp.dot(window[:, lanes], up_cols[0], preferred_element_type=F32)
        across = across + jnp.dot(beside[:, lanes], up_cols[1], preferred_element_type=F32)
        mixed[b] = jnp.dot(
            up_rows[...], across.astype(BF16), preferred_element_type=F32
        ).astype(BF16)

    store = pltpu.make_async_copy(mixed, mixed_hbm, load_sem.at[2])
    store.start()

    pan_pair(pairs - 1).wait()
    pan_map[...] += pan_pair_recv[pairs - 1].astype(F32)

    def pan_from_line(k, line):
        pan_owner(k, line, line).wait()
        pan_map[...] += pan_owner_recv[line].astype(F32)

    each_line(0, pairs - 1, pan_from_line)
    store.wait()


def local(
    pan_blocks,
    ms_blocks,
    send_list,
    tile_list,
    row_grid,
    col_grid,
    band_mix,
    band_gain,
    synth_weight,
):
    n = lax.axis_size("mrow")
    pairs = n // 2
    own_blocks, block_size, _ = pan_blocks.shape
    _, coarse_size, coarse_width = ms_blocks.shape
    slots = tile_list.shape[1]
    capacity = slots // n
    bands = band_gain.shape[0]
    pan_rows, pan_cols = KR * block_size, KC * block_size
    ms_rows, ms_cols = KR * coarse_size, KC * coarse_width
    smem = pl.BlockSpec(memory_space=pltpu.SMEM)
    vmem = pl.BlockSpec(memory_space=pltpu.VMEM)
    hbm = pl.BlockSpec(memory_space=pl.ANY)
    pan_cells, ms_cells, nodes = pl.pallas_call(
        functools.partial(cell_sums, capacity),
        grid=(n,),
        out_shape=(
            jax.ShapeDtypeStruct((n, pan_rows, pan_cols), BF16),
            jax.ShapeDtypeStruct((n, ms_rows, ms_cols), BF16),
            jax.ShapeDtypeStruct((8, 128), F32),
        ),
        in_specs=[smem, hbm, hbm, vmem, vmem],
        out_specs=(
            pl.BlockSpec((1, pan_rows, pan_cols), lambda t: (t, 0, 0)),
            pl.BlockSpec((1, ms_rows, ms_cols), lambda t: (t, 0, 0)),
            pl.BlockSpec((8, 128), lambda t: (0, 0)),
        ),
        scratch_shapes=[
            pltpu.SMEM((n * KR * KC,), jnp.int32),
            pltpu.SMEM((own_blocks,), jnp.int32),
            pltpu.VMEM(pan_blocks.shape, BF16),
            pltpu.VMEM(ms_blocks.shape, BF16),
            pltpu.SemaphoreType.DMA((2,)),
        ],
        name="cell_sums",
    )(send_list, pan_blocks, ms_blocks, row_grid[None, :], col_grid)

    coarse_rows, coarse_cols = TR // 4, TC // 4
    dma = pltpu.SemaphoreType.DMA
    ms_slots = pltpu.VMEM((pairs, 2 * coarse_rows, pan_cols), BF16)
    pan_slots = pltpu.VMEM((pairs, TR, TC), BF16)
    mixed, pan_map = pl.pallas_call(
        functools.partial(mapping, col_grid.shape[1]),
        out_shape=(
            jax.ShapeDtypeStruct((bands, TR, TC), BF16),
            jax.ShapeDtypeStruct((TR, TC), F32),
        ),
        in_specs=[vmem, hbm, hbm, smem, smem, smem],
        out_specs=(hbm, vmem),
        scratch_shapes=[
            pltpu.VMEM((n, pan_rows, pan_cols), BF16),
            pltpu.VMEM((n, ms_rows, ms_cols), BF16),
            pltpu.VMEM((2, n, 8, 128), F32),
            ms_slots,
            ms_slots,
            ms_slots,
            ms_slots,
            pan_slots,
            pan_slots,
            pan_slots,
            pan_slots,
            pltpu.VMEM((2 * coarse_rows, pan_cols), F32),
            pltpu.VMEM((pan_cols, TC), BF16),
            pltpu.VMEM((ms_cols, bands * coarse_cols), BF16),
            pltpu.VMEM((2 * coarse_rows, bands * coarse_cols), BF16),
            pltpu.VMEM((2 * coarse_rows, bands * coarse_cols), BF16),
            pltpu.VMEM((2, coarse_cols, TC), BF16),
            pltpu.VMEM((TR, 2 * coarse_rows), BF16),
            pltpu.VMEM((bands, TR, TC), BF16),
            dma((3,)),
            dma((2, n)),
            dma((2, n)),
        ]
        + [dma((pairs,))] * 8
        + [dma((5,)), dma((5,))],
        compiler_params=pltpu.CompilerParams(
            collective_id=0, has_side_effects=True, vmem_limit_bytes=60 * 1024 * 1024
        ),
        name="mapping",
    )(nodes, pan_cells, ms_cells, band_mix, band_gain, synth_weight)
    detail = band_gain[:, None, None] * pan_map[None]
    return (mixed.astype(F32) + detail).astype(BF16)


def solution(mesh):
    return jax.shard_map(
        local,
        mesh=mesh,
        in_specs=(
            P(("scene", "mrow", "mcol"), None, None),
            P(("scene", "mrow", "mcol"), None, None),
            P(None, ("scene", "mrow", "mcol")),
            P(None, ("scene", "mrow", "mcol")),
            P(("scene", "mrow")),
            P(("scene", "mrow"), "mcol"),
            P(),
            P(),
            P(),
        ),
        out_specs=P(None, ("scene", "mrow"), "mcol"),
        check_vma=False,
    )
```

profile of v0, /device:TPU:15, one launch (start us, length us, event | category | flops | bytes accessed | tf_op | source)
XLA Modules:
  0.0 49.5 jit_solution(4221910485549029254)
XLA Ops:
  0.0 6.9 %cell_sums.1 = (bf16[8,256,640]{2,1,0:T(8,128)(2,1)}, bf16[8,64,1280]{2,1,0:T(8,128)(2,1)}, f32[8,128]{1,0:T(8,128)}) custom-call(s32[3,64]{1,0:T(4,128)} %send_ref.1, bf16[64,128,128]{2,1,0:T(8,128)(2,1)} %pan_hbm.1, bf16[64,32,256]{2,1,0:T(8,128)(2,1)} %ms_hbm.1, f32[1,3]{1,0:T(1,128)} %bitcast.1, f32[1,8]{1,0:T(1,128)} %col_ref.1), custom_call_target="tpu_custom_call" | custom-call | tf_op jit(solution)/shard_map/cell_sums/pallas_call | solution.py:492
  6.9 0.0 copy-start
  6.9 40.0 %mapping.1 = (bf16[8,128,512]{2,1,0:T(8,128)(2,1)}, f32[128,512]{1,0:T(8,128)}) custom-call(f32[8,128]{1,0:T(8,128)} %get-tuple-element.10.nodes_ref, bf16[8,256,640]{2,1,0:T(8,128)(2,1)} %get-tuple-element.11.pan_hbm, bf16[8,64,1280]{2,1,0:T(8,128)(2,1)} %get-tuple-element.12.ms_hbm, f32[8,8]{1,0:T(8,128)} %mix_ref.1, f32[8]{0:T(128)} %gain_ref.1, f32[8]{0:T(128)} %synth_ref.1), custom_call_target="tpu_custom_call" | custom-call | tf_op jit(solution)/shard_map/mapping/pallas_call | solution.py:520
  46.9 0.0 copy-done
  46.9 2.6 %add_convert_fusion = bf16[8,128,512]{2,1,0:T(8,128)(2,1)} fusion(bf16[8,128,512]{2,1,0:T(8,128)(2,1)} %get-tuple-element.13, f32[128,512]{1,0:T(8,128)} %get-tuple-element.14, f32[8]{0:T(128)S(1)} %copy-done), kind=kLoop, calls=%fused_computation | loop fusion | flops 2097152 | bytes 2359328 | tf_op jit(solution)/shard_map/convert_element_type | solution.py:560
Async XLA Ops:
  6.9 40.0 %copy-start = (f32[8]{0:T(128)S(1)}, f32[8]{0:T(128)}, u32[]{:S(2)}) copy-start(f32[8]{0:T(128)} %gain_ref.1) | copy-start | bytes 100
where the time goes:
time: 49.7 us; the launch traced here: 49.5 us
  Pallas kernels  46.9 us (94%)
  other arithmetic  2.61 us (5%)
    pallas_call x1, Pallas kernels, local(): pl.pallas_call(functools.partial(mapping, col_grid.shape[1]), out_shape=(...  40 us
    pallas_call x1, Pallas kernels, local(): pl.pallas_call(functools.partial(cell_sums, capacity), grid=(n,), out_sha...  6.91 us
    convert_element_type x1, other arithmetic, local(): return (mixed.astype(F32) + detail).astype(BF16)  2.61 us

commit v1 on v0

v1 whole, which is shorter than its diff:
```python
import functools

import jax
import jax.numpy as jnp
from jax import lax
from jax.experimental import pallas as pl
from jax.experimental.pallas import tpu as pltpu
from jax.sharding import PartitionSpec as P

GRID = 64
TR = 128
TC = 512
KR = 2
KC = 5
LANES = 128
PACK = 16
HALVES = 2
MESH = pl.DeviceIdType.MESH
F32 = jnp.float32
BF16 = jnp.bfloat16
I32 = jnp.int32


def cubic_weight(offset):
    outer = jnp.maximum(2.0 - jnp.abs(offset), 0.0)
    shifted = outer - 1.0
    inner = jnp.maximum(shifted, 0.0)
    return outer * outer * (0.5 * shifted) + inner * inner * (1.0 - 2.0 * inner)


def iota(shape, dim):
    return lax.broadcasted_iota(I32, shape, dim)


def row_coord(nodes, position, offset):
    first = position < GRID
    a = jnp.where(first, nodes[0:1, 0:1], nodes[0:1, 1:2])
    b = jnp.where(first, nodes[0:1, 1:2], nodes[0:1, 2:3])
    within = (jnp.where(first, position, position - GRID).astype(F32) + offset) / GRID
    return a + (b - a) * within


def col_coord(nodes, after, is_last, count, position, offset):
    segment = position // GRID
    coord = jnp.zeros(position.shape, F32)
    for s in range(count):
        left, shift = nodes[1:2, s : s + 1], s * GRID
        if s + 1 < count:
            right = nodes[1:2, s + 1 : s + 2]
        else:
            right = jnp.where(is_last, left, after)
            left = jnp.where(is_last, nodes[1:2, s - 1 : s], left)
            shift = jnp.where(is_last, shift - GRID, shift)
        within = ((position - shift).astype(F32) + offset) / GRID
        coord = jnp.where(segment == s, left + (right - left) * within, coord)
    return coord


def mapping(
    capacity,
    col_nodes,
    send_ref,
    row_ref,
    col_ref,
    pan_hbm,
    ms_hbm,
    mix_ref,
    gain_ref,
    synth_ref,
    out_ref,
    pan_ref,
    ms_ref,
    pan_sum,
    ms_sum,
    table_ref,
    table,
    nodes_ref,
    nodes_all,
    ms_y_send,
    ms_y_recv,
    pan_y_send,
    pan_y_recv,
    ms_z_send,
    ms_z_recv,
    pan_z_send,
    pan_z_recv,
    ms_total,
    pan_total,
    col_weight,
    ms_col_weight,
    window,
    beside,
    up_cols,
    up_rows,
    mixed,
    load_sem,
    nodes_ss,
    nodes_rs,
    ms_y_ss,
    ms_y_rs,
    pan_y_ss,
    pan_y_rs,
    ms_z_ss,
    ms_z_rs,
    pan_z_ss,
    pan_z_rs,
    halo_ss,
    halo_rs,
):
    n = lax.axis_size("mrow")
    lines = n // 2
    blocks = lines // 2
    scene = lax.axis_index("scene")
    m = lax.axis_index("mrow")
    c = lax.axis_index("mcol")
    z, y = m // 2, m % 2
    twin = z * 2 + (1 - y)
    other = 1 - c
    pair = z // 2
    partner = pair * 2 + (1 - z % 2)
    own_blocks, size, _ = pan_ref.shape
    _, coarse_size, coarse_width = ms_ref.shape
    cells = n * KR * KC
    bands = mixed.shape[0]
    coarse_rows = TR // 4
    coarse_cols = TC // 4
    half = coarse_rows // 2
    mid = half + coarse_rows
    part_rows = TR // HALVES
    first_col = c * KC
    is_last = c == lax.axis_size("mcol") - 1

    def at(row, col):
        return (scene, row, col)

    def remote(src, dst, ss, rs, row, col):
        return pltpu.make_async_remote_copy(
            src_ref=src,
            dst_ref=dst,
            send_sem=ss,
            recv_sem=rs,
            device_id=at(row, col),
            device_id_type=MESH,
        )

    barrier = pltpu.get_barrier_semaphore()

    def greet(k, carry):
        row = lax.rem(m + k, n)
        pl.semaphore_signal(barrier, inc=1, device_id=at(row, c), device_id_type=MESH)
        pl.semaphore_signal(barrier, inc=1, device_id=at(row, other), device_id_type=MESH)
        return carry

    pl.semaphore_signal(barrier, inc=1, device_id=at(m, other), device_id_type=MESH)
    lax.fori_loop(1, n, greet, 0)
    ms_load = pltpu.make_async_copy(ms_hbm, ms_ref, load_sem.at[0])
    pan_load = pltpu.make_async_copy(pan_hbm, pan_ref, load_sem.at[1])
    ms_load.start()
    pan_load.start()

    nodes_ref[...] = jnp.zeros_like(nodes_ref)
    nodes_ref[0:1, 0 : row_ref.shape[1]] = row_ref[...]
    nodes_ref[1:2, 0 : col_ref.shape[1]] = col_ref[...]
    nodes_all[c, m] = nodes_ref[...]

    square = (own_blocks, own_blocks)
    wide = (own_blocks, LANES)
    owner = send_ref[0:1, :] // capacity
    key_row = (owner * KR + send_ref[1:2, :]) * KC + send_ref[2:3, :] - first_col
    key_row = jnp.broadcast_to(key_row, square)
    diagonal = iota(square, 0) == iota(square, 1)
    key_col = jnp.sum(jnp.where(diagonal, key_row, 0), axis=1, keepdims=True)
    same = key_row == key_col
    before = (key_row < key_col) | (same & (iota(square, 1) < iota(square, 0)))
    rank = jnp.sum(jnp.where(before, 1, 0), axis=1, keepdims=True)
    joined = jnp.sum(jnp.where(before & same, 1, 0), axis=1, keepdims=True)
    hit = rank == iota(wide, 1)
    order = jnp.sum(jnp.where(hit, iota(wide, 0), 0), axis=0, keepdims=True)
    keep = jnp.sum(jnp.where(hit & (joined > 0), 1, 0), axis=0, keepdims=True)
    table_ref[0:1, :] = order
    table_ref[1:2, :] = keep
    for g in range(pl.cdiv(cells, LANES)):
        cell = iota(wide, 1) + g * LANES
        ends = jnp.sum(jnp.where(key_col <= cell, 1, 0), axis=0, keepdims=True)
        count = jnp.sum(jnp.where(key_col == cell, 1, 0), axis=0, keepdims=True)
        table_ref[2 + g : 3 + g, :] = jnp.where(count > 0, ends, 0)
    table_copy = pltpu.make_async_copy(table_ref, table, load_sem.at[2])
    table_copy.start()

    tap = iota((TR, 2 * coarse_rows), 1) - (half - 2)
    spot = (iota((TR, 2 * coarse_rows), 0).astype(F32) - 1.5) * 0.25 + 2.0
    up_rows[...] = cubic_weight(spot - tap.astype(F32)).astype(BF16)
    ms_col_weight[...] = jnp.zeros_like(ms_col_weight)
    pan_sum[0] = jnp.zeros((size, size), BF16)
    ms_sum[0] = jnp.zeros((coarse_size, coarse_width), BF16)
    pl.semaphore_wait(barrier, 2 * n - 1)

    def nodes_copy(slot_row, slot_col, row, col):
        return remote(
            nodes_ref,
            nodes_all.at[slot_col, slot_row],
            nodes_ss.at[col, row],
            nodes_rs.at[slot_col, slot_row],
            row,
            col,
        )

    def send_nodes(k, carry):
        row = lax.rem(m + k, n)
        nodes_copy(m, c, row, c).start()
        nodes_copy(m, c, row, other).start()
        return carry

    lax.fori_loop(1, n, send_nodes, 0)
    nodes_copy(m, c, m, other).start()
    table_copy.wait()

    def running(source, sums):
        def step(p, total):
            total = total * table[1, p].astype(F32) + source[table[0, p]].astype(F32)
            sums[p + 1] = total.astype(BF16)
            return total

        start = jnp.zeros(source.shape[1:], F32)
        lax.fori_loop(0, own_blocks, step, start, unroll=2)

    ms_load.wait()
    running(ms_ref, ms_sum)
    pan_load.wait()
    running(pan_ref, pan_sum)

    def wait_nodes(k, carry):
        row = lax.rem(m + k, n)
        nodes_copy(row, c, row, c).wait()
        nodes_copy(row, other, row, other).wait()
        return carry

    lax.fori_loop(1, n, wait_nodes, 0)
    nodes_copy(m, other, m, other).wait()

    def cell_of(sums, tile, row, col):
        cell = (tile * KR + row) * KC + col
        return sums[table[2 + cell // LANES, cell % LANES]]

    def stacked(sums, tile, col):
        return jnp.concatenate([cell_of(sums, tile, row, col) for row in range(KR)], axis=0)

    def ms_part(tile):
        nodes = nodes_all[c, tile]
        after = nodes_all[1, tile][1:2, 0:1]
        x_ms = col_coord(
            nodes, after, is_last, col_nodes, 4 * iota((1, coarse_cols), 1) + 1, 0.5
        )
        x_ms = (x_ms - 1.5) * 0.25
        for k in range(KC):
            pixel = (first_col + k) * coarse_size + iota((coarse_size, coarse_cols), 0)
            weight = cubic_weight(x_ms - pixel.astype(F32)).astype(BF16)
            for b in range(bands):
                row = (k * bands + b) * coarse_size
                lanes = slice(b * coarse_cols, (b + 1) * coarse_cols)
                ms_col_weight[row : row + coarse_size, lanes] = weight
        spots = (row_coord(nodes, 4 * iota((coarse_rows, 1), 0) + 1, 0.5) - 1.5) * 0.25
        taps = iota((coarse_rows, KR * coarse_size), 1).astype(F32)
        weight = cubic_weight(spots - taps).astype(BF16)
        rows = [
            jnp.dot(weight, stacked(ms_sum, tile, k), preferred_element_type=F32).astype(BF16)
            for k in range(KC)
        ]
        return jnp.dot(
            jnp.concatenate(rows, axis=1), ms_col_weight[...], preferred_element_type=F32
        )

    def pan_part(tile):
        nodes = nodes_all[c, tile]
        after = nodes_all[1, tile][1:2, 0:1]
        x_pan = col_coord(nodes, after, is_last, col_nodes, iota((1, TC), 1), 0.0)
        base = jnp.floor(x_pan)
        taps = [
            jnp.broadcast_to(cubic_weight(x_pan - (base + float(t))), (PACK, TC)).astype(BF16)
            for t in range(-1, 3)
        ]
        none = jnp.zeros((PACK, TC), BF16)
        for k in range(KC):
            origin = ((first_col + k) * size).astype(F32)
            begin = jnp.clip(base - origin, -4.0, size + 3.0)
            away = (iota((PACK, TC), 0).astype(F32) - begin).astype(BF16)
            for g in range(size // PACK):
                value = none
                for t in range(4):
                    value = jnp.where(away == BF16(t - 1 - g * PACK), taps[t], value)
                row = k * size + g * PACK
                col_weight[row : row + PACK, :] = value
        spots = row_coord(nodes, iota((TR, 1), 0), 0.0)
        pixels = iota((TR, KR * size), 1).astype(F32)
        weight = cubic_weight(spots - pixels).astype(BF16)
        rows = [
            jnp.dot(weight, stacked(pan_sum, tile, k), preferred_element_type=F32).astype(BF16)
            for k in range(KC)
        ]
        return jnp.dot(jnp.concatenate(rows, axis=1), col_weight[...], preferred_element_type=F32)

    def line_of(k):
        up = lax.rem(pair * 2 + 2 + k, lines)
        down = lax.rem(pair * 2 + lines - 1 - k, lines)
        far = jnp.where(pair % 2 == 0, down, up)
        return jnp.where(k < lines - 2, far, jnp.where(k == lines - 2, partner, z))

    def ms_y(k):
        return remote(ms_y_send.at[k], ms_y_recv.at[k], ms_y_ss.at[k], ms_y_rs.at[k], twin, c)

    def pan_y(k, h):
        part = pl.ds(h * part_rows, part_rows)
        return remote(
            pan_y_send.at[k, part],
            pan_y_recv.at[k, part],
            pan_y_ss.at[k, h],
            pan_y_rs.at[k, h],
            twin,
            c,
        )

    def route(line):
        far = line // 2 != pair
        above = line // 2 > pair
        lower = z % 2 == 0
        inner = far & jnp.logical_xor(above, lower)
        outer = far & jnp.logical_not(jnp.logical_xor(above, lower))
        target = jnp.where(outer, partner, line)
        slot = jnp.where(outer, blocks + line, pair)
        return inner, target * 2 + y, slot

    def ms_z(k, row, slot):
        return remote(
            ms_z_send.at[k], ms_z_recv.at[slot], ms_z_ss.at[k], ms_z_rs.at[slot], row, c
        )

    def pan_z(k, h, row, slot):
        part = pl.ds(h * part_rows, part_rows)
        return remote(
            pan_z_send.at[k, part],
            pan_z_recv.at[slot, part],
            pan_z_ss.at[k, h],
            pan_z_rs.at[slot, h],
            row,
            c,
        )

    def each(first, last, step):
        def body(k, carry):
            step(k, line_of(k))
            return carry

        lax.fori_loop(first, last, body, 0)

    def ms_to_twin(k, line):
        ms_y_send[k] = ms_part(line * 2 + 1 - y).astype(BF16)
        ms_y(k).start()

    def pan_to_twin(k, line):
        pan_y_send[k] = pan_part(line * 2 + 1 - y).astype(BF16)
        for h in range(HALVES):
            pan_y(k, h).start()

    def ms_onward(k, line):
        inner, row, slot = route(line)
        ms_total[...] = ms_part(line * 2 + y)
        ms_y(k).wait_recv()
        ms_total[...] += ms_y_recv[k].astype(F32)

        @pl.when(inner)
        def _():
            ms_z(0, row, blocks + line).wait_recv()
            ms_total[...] += ms_z_recv[blocks + line].astype(F32)

        ms_z_send[k] = ms_total[...].astype(BF16)
        ms_z(k, row, slot).start()

    def pan_onward(k, line):
        inner, row, slot = route(line)
        pan_total[...] = pan_part(line * 2 + y)
        for h in range(HALVES):
            rows = slice(h * part_rows, (h + 1) * part_rows)
            pan_y(k, h).wait_recv()
            pan_total[rows, :] += pan_y_recv[k, rows].astype(F32)

            @pl.when(inner)
            def _():
                pan_z(0, h, row, blocks + line).wait_recv()
                pan_total[rows, :] += pan_z_recv[blocks + line, rows].astype(F32)

            pan_z_send[k, rows] = pan_total[rows, :].astype(BF16)
            pan_z(k, h, row, slot).start()

    each(0, lines, ms_to_twin)
    each(0, 2, pan_to_twin)
    each(0, lines - 1, ms_onward)
    each(2, lines, pan_to_twin)

    spot = (iota((coarse_cols, TC), 1).astype(F32) - 1.5) * 0.25 + 2.0
    tap = iota((coarse_cols, TC), 0) + 2
    up_cols[0:coarse_cols, :] = cubic_weight(spot - tap.astype(F32)).astype(BF16)
    tap = tap + jnp.where(c == 0, coarse_cols, -coarse_cols)
    up_cols[coarse_cols : 2 * coarse_cols, :] = cubic_weight(spot - tap.astype(F32)).astype(BF16)

    each(0, 1, pan_onward)

    ms_total[...] = ms_part(m)
    ms_y(lines - 1).wait_recv()
    ms_total[...] += ms_y_recv[lines - 1].astype(F32)

    def ms_arrived(slot, carry):
        ms_z(0, m, slot).wait_recv()
        ms_total[...] += ms_z_recv[slot].astype(F32)
        return carry

    lax.fori_loop(0, blocks, ms_arrived, 0)
    values = [ms_total[:, b * coarse_cols : (b + 1) * coarse_cols] for b in range(bands)]
    synthetic = sum(synth_ref[b] * values[b] for b in range(bands))
    for b in range(bands):
        result = values[b] - gain_ref[b] * synthetic
        for k in range(bands):
            result = result + mix_ref[b, k] * values[k]
        window[half:mid, b * coarse_cols : (b + 1) * coarse_cols] = result.astype(BF16)

    has_above, has_below = m > 0, m < n - 1

    def halo_copy(k, src, rows, dst, start, row, col):
        return remote(
            window.at[pl.ds(src, rows)],
            dst.at[pl.ds(start, rows)],
            halo_ss.at[k],
            halo_rs.at[k],
            row,
            col,
        )

    across_copy = halo_copy(0, half, coarse_rows, beside, half, m, other)
    up_copies = [
        halo_copy(1, half, half, window, mid, m - 1, c),
        halo_copy(2, half, half, beside, mid, m - 1, other),
    ]
    down_copies = [
        halo_copy(3, coarse_rows, half, window, 0, m + 1, c),
        halo_copy(4, coarse_rows, half, beside, 0, m + 1, other),
    ]
    across_copy.start()

    @pl.when(has_above)
    def _():
        for copy in up_copies:
            copy.start()

    @pl.when(has_below)
    def _():
        for copy in down_copies:
            copy.start()

    each(1, lines - 1, pan_onward)
    pan_total[...] = pan_part(m)
    across_copy.wait()

    @pl.when(has_above)
    def _():
        for copy in up_copies:
            copy.wait_send()
        for copy in down_copies:
            copy.wait_recv()

    @pl.when(has_below)
    def _():
        for copy in down_copies:
            copy.wait_send()
        for copy in up_copies:
            copy.wait_recv()

    edge = jnp.zeros((half, window.shape[1]), BF16)

    @pl.when(jnp.logical_not(has_above))
    def _():
        window[0:half, :] = edge
        beside[0:half, :] = edge

    @pl.when(jnp.logical_not(has_below))
    def _():
        window[mid : mid + half, :] = edge
        beside[mid : mid + half, :] = edge

    for b in range(bands):
        lanes = slice(b * coarse_cols, (b + 1) * coarse_cols)
        source = jnp.concatenate([window[:, lanes], beside[:, lanes]], axis=1)
        across = jnp.dot(source, up_cols[...], preferred_element_type=F32)
        mixed[b] = jnp.dot(up_rows[...], across.astype(BF16), preferred_element_type=F32)

    for h in range(HALVES):
        rows = slice(h * part_rows, (h + 1) * part_rows)
        pan_y(lines - 1, h).wait_recv()
        pan_total[rows, :] += pan_y_recv[lines - 1, rows].astype(F32)

        def pan_arrived(slot, carry):
            pan_z(0, h, m, slot).wait_recv()
            pan_total[rows, :] += pan_z_recv[slot, rows].astype(F32)
            return carry

        lax.fori_loop(0, blocks, pan_arrived, 0)
        for b in range(bands):
            out_ref[b, rows, :] = (mixed[b, rows, :] + gain_ref[b] * pan_total[rows, :]).astype(
                BF16
            )

    def y_sent(k, carry):
        ms_y(k).wait_send()
        for h in range(HALVES):
            pan_y(k, h).wait_send()
        return carry

    def z_sent(k, carry):
        ms_z(k, m, 0).wait_send()
        for h in range(HALVES):
            pan_z(k, h, m, 0).wait_send()
        return carry

    lax.fori_loop(0, lines, y_sent, 0)
    lax.fori_loop(0, lines - 1, z_sent, 0)


def local(
    pan_blocks,
    ms_blocks,
    send_list,
    tile_list,
    row_grid,
    col_grid,
    band_mix,
    band_gain,
    synth_weight,
):
    n = lax.axis_size("mrow")
    lines = n // 2
    own_blocks, size, _ = pan_blocks.shape
    _, coarse_size, coarse_width = ms_blocks.shape
    capacity = tile_list.shape[1] // n
    bands = band_gain.shape[0]
    coarse_rows, coarse_cols = TR // 4, TC // 4
    ms_width = bands * coarse_cols
    table_rows = pl.cdiv(2 + pl.cdiv(n * KR * KC, LANES), 8) * 8
    smem = pl.BlockSpec(memory_space=pltpu.SMEM)
    vmem = pl.BlockSpec(memory_space=pltpu.VMEM)
    hbm = pl.BlockSpec(memory_space=pl.ANY)
    dma = pltpu.SemaphoreType.DMA
    slots = lines // 2 + lines

    def ms_slots(count):
        return pltpu.VMEM((count, coarse_rows, ms_width), BF16)

    def pan_slots(count):
        return pltpu.VMEM((count, TR, TC), BF16)

    return pl.pallas_call(
        functools.partial(mapping, capacity, col_grid.shape[1]),
        out_shape=jax.ShapeDtypeStruct((bands, TR, TC), BF16),
        in_specs=[vmem, vmem, vmem, hbm, hbm, smem, smem, smem],
        out_specs=vmem,
        scratch_shapes=[
            pltpu.VMEM(pan_blocks.shape, BF16),
            pltpu.VMEM(ms_blocks.shape, BF16),
            pltpu.VMEM((own_blocks + 1, size, size), BF16),
            pltpu.VMEM((own_blocks + 1, coarse_size, coarse_width), BF16),
            pltpu.VMEM((table_rows, LANES), I32),
            pltpu.SMEM((table_rows, LANES), I32),
            pltpu.VMEM((8, LANES), F32),
            pltpu.VMEM((2, n, 8, LANES), F32),
            ms_slots(lines),
            ms_slots(lines),
            pan_slots(lines),
            pan_slots(lines),
            ms_slots(lines - 1),
            ms_slots(slots),
            pan_slots(lines - 1),
            pan_slots(slots),
            pltpu.VMEM((coarse_rows, ms_width), F32),
            pltpu.VMEM((TR, TC), F32),
            pltpu.VMEM((KC * size, TC), BF16),
            pltpu.VMEM((KC * bands * coarse_size, ms_width), BF16),
            pltpu.VMEM((2 * coarse_rows, ms_width), BF16),
            pltpu.VMEM((2 * coarse_rows, ms_width), BF16),
            pltpu.VMEM((2 * coarse_cols, TC), BF16),
            pltpu.VMEM((TR, 2 * coarse_rows), BF16),
            pltpu.VMEM((bands, TR, TC), F32),
            dma((3,)),
            dma((2, n)),
            dma((2, n)),
            dma((lines,)),
            dma((lines,)),
            dma((lines, HALVES)),
            dma((lines, HALVES)),
            dma((lines - 1,)),
            dma((slots,)),
            dma((lines - 1, HALVES)),
            dma((slots, HALVES)),
            dma((5,)),
            dma((5,)),
        ],
        compiler_params=pltpu.CompilerParams(
            collective_id=0, has_side_effects=True, vmem_limit_bytes=40 * 1024 * 1024
        ),
        name="mapping",
    )(
        send_list,
        row_grid[None, :],
        col_grid,
        pan_blocks,
        ms_blocks,
        band_mix,
        band_gain,
        synth_weight,
    )


def solution(mesh):
    return jax.shard_map(
        local,
        mesh=mesh,
        in_specs=(
            P(("scene", "mrow", "mcol"), None, None),
            P(("scene", "mrow", "mcol"), None, None),
            P(None, ("scene", "mrow", "mcol")),
            P(None, ("scene", "mrow", "mcol")),
            P(("scene", "mrow")),
            P(("scene", "mrow"), "mcol"),
            P(),
            P(),
            P(),
        ),
        out_specs=P(None, ("scene", "mrow"), "mcol"),
        check_vma=False,
    )
```

time: 49.7 us -> 45 us (0.905)
  the two profiles are of different devices: /device:TPU:15 before, /device:TPU:0 now
where the time goes in v1:
time: 45 us; the launch traced here: 44.6 us
  Pallas kernels  36.8 us (82%)
  local copies, waits for them, and re-layouts  7.77 us (17%)
    pallas_call x1, Pallas kernels, local(): pl.pallas_call(functools.partial(mapping, capacity, col_grid.shape[1]), o...  36.8 us
    unnamed x17, local copies, waits for them, and re-layouts  7.77 us

profile of v1, /device:TPU:0, one launch (start us, length us, event | category | flops | bytes accessed | tf_op | source)
XLA Modules:
  0.0 44.6 jit_solution(9437843174952674056)
XLA Ops:
  0.0 0.0 copy-start
  0.0 1.6 %copy-done = bf16[64,128,128]{2,1,0:T(8,128)(2,1)S(1)} copy-done((bf16[64,128,128]{2,1,0:T(8,128)(2,1)S(1)}, bf16[64,128,128]{2,1,0:T(8,128)(2,1)}, u32[]{:S(2)}) %copy-start) | copy-done | bytes 2097176
  1.6 0.0 copy-start.1
  1.6 1.2 %copy-done.1 = bf16[64,32,256]{2,1,0:T(8,128)(2,1)S(1)} copy-done((bf16[64,32,256]{2,1,0:T(8,128)(2,1)S(1)}, bf16[64,32,256]{2,1,0:T(8,128)(2,1)}, u32[]{:S(2)}) %copy-start.1) | copy-done | bytes 1048600
  2.8 0.0 copy-start.2
  2.8 0.7 %copy-done.2 = f32[8,8]{1,0:T(8,128)S(1)} copy-done((f32[8,8]{1,0:T(8,128)S(1)}, f32[8,8]{1,0:T(8,128)}, u32[]{:S(2)}) %copy-start.2) | copy-done | bytes 280
  3.5 0.0 copy-start.3
  3.5 0.7 %copy-done.3 = s32[3,64]{1,0:T(4,128)S(1)} copy-done((s32[3,64]{1,0:T(4,128)S(1)}, s32[3,64]{1,0:T(4,128)}, u32[]{:S(2)}) %copy-start.3) | copy-done | bytes 792
  4.2 0.0 copy-start.4
  4.2 0.7 %copy-done.4 = f32[3]{0:T(128)S(1)} copy-done((f32[3]{0:T(128)S(1)}, f32[3]{0:T(128)}, u32[]{:S(2)}) %copy-start.4) | copy-done | bytes 36
  4.8 0.0 copy-start.5
  4.8 0.7 %copy-done.5 = f32[1,8]{1,0:T(1,128)S(1)} copy-done((f32[1,8]{1,0:T(1,128)S(1)}, f32[1,8]{1,0:T(1,128)}, u32[]{:S(2)}) %copy-start.5) | copy-done | bytes 56
  5.5 0.0 copy-start.6
  5.5 0.7 %copy-done.6 = f32[8]{0:T(128)S(1)} copy-done((f32[8]{0:T(128)S(1)}, f32[8]{0:T(128)}, u32[]{:S(2)}) %copy-start.6) | copy-done | bytes 56
  6.2 0.0 copy-start.7
  6.2 0.7 %copy-done.7 = f32[8]{0:T(128)S(1)} copy-done((f32[8]{0:T(128)S(1)}, f32[8]{0:T(128)}, u32[]{:S(2)}) %copy-start.7) | copy-done | bytes 56
  6.8 36.8 %mapping.1 = bf16[8,128,512]{2,1,0:T(8,128)(2,1)S(1)} custom-call(s32[3,64]{1,0:T(4,128)S(1)} %copy-done.3, f32[1,3]{1,0:T(1,128)S(1)} %bitcast.1, f32[1,8]{1,0:T(1,128)S(1)} %copy-done.5, bf16[64,128,128]{2,1,0:T(8,128)(2,1)S(1)} %copy-done, bf16[64,32,256]{2,1,0:T(8,128)(2,1)S(1)} %copy-done.1, f32[8,8]{1,0:T(8,128)S(1)} %copy-done.2, f32[8]{0:T(128)S(1)} %copy-done.6, ...), custom_call_target="tpu_custom_call" | custom-call | tf_op jit(solution)/shard_map/mapping/pallas_call | solution.py:558
  43.6 1.0 %copy.10 = bf16[8,128,512]{2,1,0:T(8,128)(2,1)} copy(bf16[8,128,512]{2,1,0:T(8,128)(2,1)S(1)} %mapping.1) | data formatting | bytes 2097152
Async XLA Ops:
  0.0 1.6 %copy-start = (bf16[64,128,128]{2,1,0:T(8,128)(2,1)S(1)}, bf16[64,128,128]{2,1,0:T(8,128)(2,1)}, u32[]{:S(2)}) copy-start(bf16[64,128,128]{2,1,0:T(8,128)(2,1)} %pan_hbm.1) | copy-start | bytes 6291460
  1.6 1.2 %copy-start.1 = (bf16[64,32,256]{2,1,0:T(8,128)(2,1)S(1)}, bf16[64,32,256]{2,1,0:T(8,128)(2,1)}, u32[]{:S(2)}) copy-start(bf16[64,32,256]{2,1,0:T(8,128)(2,1)} %ms_hbm.1) | copy-start | bytes 3145732
  2.8 0.7 %copy-start.2 = (f32[8,8]{1,0:T(8,128)S(1)}, f32[8,8]{1,0:T(8,128)}, u32[]{:S(2)}) copy-start(f32[8,8]{1,0:T(8,128)} %mix_ref.1) | copy-start | bytes 772
  3.5 0.7 %copy-start.3 = (s32[3,64]{1,0:T(4,128)S(1)}, s32[3,64]{1,0:T(4,128)}, u32[]{:S(2)}) copy-start(s32[3,64]{1,0:T(4,128)} %send_ref.1) | copy-start | bytes 2308
  4.2 0.7 %copy-start.4 = (f32[3]{0:T(128)S(1)}, f32[3]{0:T(128)}, u32[]{:S(2)}) copy-start(f32[3]{0:T(128)} %param.12) | copy-start | bytes 40
  4.8 0.7 %copy-start.5 = (f32[1,8]{1,0:T(1,128)S(1)}, f32[1,8]{1,0:T(1,128)}, u32[]{:S(2)}) copy-start(f32[1,8]{1,0:T(1,128)} %col_ref.1) | copy-start | bytes 100
  5.5 0.7 %copy-start.6 = (f32[8]{0:T(128)S(1)}, f32[8]{0:T(128)}, u32[]{:S(2)}) copy-start(f32[8]{0:T(128)} %gain_ref.1) | copy-start | bytes 100
  6.2 0.7 %copy-start.7 = (f32[8]{0:T(128)S(1)}, f32[8]{0:T(128)}, u32[]{:S(2)}) copy-start(f32[8]{0:T(128)} %synth_ref.1) | copy-start | bytes 100

commit v2 on v1

--- a/solution.py
+++ b/solution.py
@@ -15,6 +15,7 @@
 LANES = 128
 PACK = 16
 HALVES = 2
+GROUP = 4
 MESH = pl.DeviceIdType.MESH
 F32 = jnp.float32
 BF16 = jnp.bfloat16
@@ -56,18 +57,49 @@
     return coord
 
 
+def spread(x, origin, size):
+    base = jnp.floor(x)
+    shape = (PACK, x.shape[1])
+    taps = [
+        jnp.broadcast_to(cubic_weight(x - (base + t)), shape).astype(BF16)
+        for t in (-1.0, 0.0, 1.0, 2.0)
+    ]
+    groups = size // PACK
+    first = base - 1.0 - origin
+    group = jnp.floor(first * (1.0 / PACK))
+    away = (iota(shape, 0).astype(F32) - (first - group * PACK)).astype(BF16)
+    group = jnp.broadcast_to(jnp.clip(group, -2.0, groups + 1.0), shape).astype(BF16)
+    none = jnp.zeros(shape, BF16)
+    low, high = none, none
+    for t in range(4):
+        low = jnp.where(away == BF16(t), taps[t], low)
+        high = jnp.where(away == BF16(t - PACK), taps[t], high)
+    here = [group == BF16(g) for g in range(-1, groups)]
+    return jnp.concatenate(
+        [jnp.where(here[g + 1], low, jnp.where(here[g], high, none)) for g in range(groups)],
+        axis=0,
+    )
+
+
 def mapping(
     capacity,
     col_nodes,
+    send_hbm,
+    row_hbm,
+    col_hbm,
+    pan_hbm,
+    ms_hbm,
+    mix_hbm,
+    gain_hbm,
+    synth_hbm,
+    mixed_hbm,
+    pan_total,
     send_ref,
     row_ref,
     col_ref,
-    pan_hbm,
-    ms_hbm,
     mix_ref,
     gain_ref,
     synth_ref,
-    out_ref,
     pan_ref,
     ms_ref,
     pan_sum,
@@ -85,11 +117,9 @@
     pan_z_send,
     pan_z_recv,
     ms_total,
-    pan_total,
-    col_weight,
-    ms_col_weight,
     window,
-    beside,
+    edge_own,
+    edge_all,
     up_cols,
     up_rows,
     mixed,
@@ -153,15 +183,52 @@
 
     pl.semaphore_signal(barrier, inc=1, device_id=at(m, other), device_id_type=MESH)
     lax.fori_loop(1, n, greet, 0)
-    ms_load = pltpu.make_async_copy(ms_hbm, ms_ref, load_sem.at[0])
-    pan_load = pltpu.make_async_copy(pan_hbm, pan_ref, load_sem.at[1])
-    ms_load.start()
-    pan_load.start()
+    loads = [
+        pltpu.make_async_copy(src, dst, load_sem.at[k])
+        for k, (src, dst) in enumerate(
+            (
+                (row_hbm, row_ref),
+                (col_hbm, col_ref),
+                (send_hbm, send_ref),
+                (ms_hbm, ms_ref),
+                (pan_hbm, pan_ref),
+                (mix_hbm, mix_ref),
+                (gain_hbm, gain_ref),
+                (synth_hbm, synth_ref),
+            )
+        )
+    ]
+    for load in loads:
+        load.start()
+    row_load, col_load, send_load, ms_load, pan_load, *late_loads = loads
 
     nodes_ref[...] = jnp.zeros_like(nodes_ref)
+    row_load.wait()
+    col_load.wait()
     nodes_ref[0:1, 0 : row_ref.shape[1]] = row_ref[...]
     nodes_ref[1:2, 0 : col_ref.shape[1]] = col_ref[...]
     nodes_all[c, m] = nodes_ref[...]
+    pl.semaphore_wait(barrier, 2 * n - 1)
+
+    def nodes_copy(slot_row, slot_col, row, col):
+        return remote(
+            nodes_ref,
+            nodes_all.at[slot_col, slot_row],
+            nodes_ss.at[col, row],
+            nodes_rs.at[slot_col, slot_row],
+            row,
+            col,
+        )
+
+    def send_nodes(k, carry):
+        row = lax.rem(m + k, n)
+        nodes_copy(m, c, row, c).start()
+        nodes_copy(m, c, row, other).start()
+        return carry
+
+    lax.fori_loop(1, n, send_nodes, 0)
+    nodes_copy(m, c, m, other).start()
+    send_load.wait()
 
     square = (own_blocks, own_blocks)
     wide = (own_blocks, LANES)
@@ -184,35 +251,14 @@
         ends = jnp.sum(jnp.where(key_col <= cell, 1, 0), axis=0, keepdims=True)
         count = jnp.sum(jnp.where(key_col == cell, 1, 0), axis=0, keepdims=True)
         table_ref[2 + g : 3 + g, :] = jnp.where(count > 0, ends, 0)
-    table_copy = pltpu.make_async_copy(table_ref, table, load_sem.at[2])
+    table_copy = pltpu.make_async_copy(table_ref, table, load_sem.at[8])
     table_copy.start()
 
     tap = iota((TR, 2 * coarse_rows), 1) - (half - 2)
     spot = (iota((TR, 2 * coarse_rows), 0).astype(F32) - 1.5) * 0.25 + 2.0
     up_rows[...] = cubic_weight(spot - tap.astype(F32)).astype(BF16)
-    ms_col_weight[...] = jnp.zeros_like(ms_col_weight)
     pan_sum[0] = jnp.zeros((size, size), BF16)
     ms_sum[0] = jnp.zeros((coarse_size, coarse_width), BF16)
-    pl.semaphore_wait(barrier, 2 * n - 1)
-
-    def nodes_copy(slot_row, slot_col, row, col):
-        return remote(
-            nodes_ref,
-            nodes_all.at[slot_col, slot_row],
-            nodes_ss.at[col, row],
-            nodes_rs.at[slot_col, slot_row],
-            row,
-            col,
-        )
-
-    def send_nodes(k, carry):
-        row = lax.rem(m + k, n)
-        nodes_copy(m, c, row, c).start()
-        nodes_copy(m, c, row, other).start()
-        return carry
-
-    lax.fori_loop(1, n, send_nodes, 0)
-    nodes_copy(m, c, m, other).start()
     table_copy.wait()
 
     def running(source, sums):
@@ -252,13 +298,7 @@
             nodes, after, is_last, col_nodes, 4 * iota((1, coarse_cols), 1) + 1, 0.5
         )
         x_ms = (x_ms - 1.5) * 0.25
-        for k in range(KC):
-            pixel = (first_col + k) * coarse_size + iota((coarse_size, coarse_cols), 0)
-            weight = cubic_weight(x_ms - pixel.astype(F32)).astype(BF16)
-            for b in range(bands):
-                row = (k * bands + b) * coarse_size
-                lanes = slice(b * coarse_cols, (b + 1) * coarse_cols)
-                ms_col_weight[row : row + coarse_size, lanes] = weight
+        col = spread(x_ms, (first_col * coarse_size).astype(F32), KC * coarse_size)
         spots = (row_coord(nodes, 4 * iota((coarse_rows, 1), 0) + 1, 0.5) - 1.5) * 0.25
         taps = iota((coarse_rows, KR * coarse_size), 1).astype(F32)
         weight = cubic_weight(spots - taps).astype(BF16)
@@ -266,38 +306,31 @@
             jnp.dot(weight, stacked(ms_sum, tile, k), preferred_element_type=F32).astype(BF16)
             for k in range(KC)
         ]
-        return jnp.dot(
-            jnp.concatenate(rows, axis=1), ms_col_weight[...], preferred_element_type=F32
-        )
+        by_band = [
+            jnp.concatenate(
+                [row[:, b * coarse_size : (b + 1) * coarse_size] for row in rows], axis=1
+            )
+            for b in range(bands)
+        ]
+        return jnp.dot(jnp.concatenate(by_band, axis=0), col, preferred_element_type=F32)
 
     def pan_part(tile):
         nodes = nodes_all[c, tile]
         after = nodes_all[1, tile][1:2, 0:1]
         x_pan = col_coord(nodes, after, is_last, col_nodes, iota((1, TC), 1), 0.0)
-        base = jnp.floor(x_pan)
-        taps = [
-            jnp.broadcast_to(cubic_weight(x_pan - (base + float(t))), (PACK, TC)).astype(BF16)
-            for t in range(-1, 3)
-        ]
-        none = jnp.zeros((PACK, TC), BF16)
-        for k in range(KC):
-            origin = ((first_col + k) * size).astype(F32)
-            begin = jnp.clip(base - origin, -4.0, size + 3.0)
-            away = (iota((PACK, TC), 0).astype(F32) - begin).astype(BF16)
-            for g in range(size // PACK):
-                value = none
-                for t in range(4):
-                    value = jnp.where(away == BF16(t - 1 - g * PACK), taps[t], value)
-                row = k * size + g * PACK
-                col_weight[row : row + PACK, :] = value
-        spots = row_coord(nodes, iota((TR, 1), 0), 0.0)
-        pixels = iota((TR, KR * size), 1).astype(F32)
-        weight = cubic_weight(spots - pixels).astype(BF16)
-        rows = [
-            jnp.dot(weight, stacked(pan_sum, tile, k), preferred_element_type=F32).astype(BF16)
-            for k in range(KC)
-        ]
-        return jnp.dot(jnp.concatenate(rows, axis=1), col_weight[...], preferred_element_type=F32)
+        col = spread(x_pan, (first_col * size).astype(F32), KC * size)
+        row = spread(row_coord(nodes, iota((1, TR), 1), 0.0), 0.0, KR * size)
+        rows = []
+        for k in range(0, KC, 2):
+            source = jnp.concatenate(
+                [stacked(pan_sum, tile, j) for j in range(k, min(k + 2, KC))], axis=1
+            )
+            rows.append(
+                lax.dot_general(
+                    row, source, (((0,), (0,)), ((), ())), preferred_element_type=F32
+                ).astype(BF16)
+            )
+        return jnp.dot(jnp.concatenate(rows, axis=1), col, preferred_element_type=F32)
 
     def line_of(k):
         up = lax.rem(pair * 2 + 2 + k, lines)
@@ -346,36 +379,47 @@
         )
 
     def each(first, last, step):
+        if last - first == 1:
+            step(first)
+            return
+
         def body(k, carry):
-            step(k, line_of(k))
+            step(k)
             return carry
 
         lax.fori_loop(first, last, body, 0)
 
-    def ms_to_twin(k, line):
-        ms_y_send[k] = ms_part(line * 2 + 1 - y).astype(BF16)
-        ms_y(k).start()
-
-    def pan_to_twin(k, line):
-        pan_y_send[k] = pan_part(line * 2 + 1 - y).astype(BF16)
+    def ms_to_twin(k):
+        parts = [ms_part(line_of(k + i) * 2 + 1 - y) for i in range(2)]
+        for i, part in enumerate(parts):
+            ms_y_send[k + i] = part.astype(BF16)
+
+    def pan_to_twin(k):
+        pan_y_send[k] = pan_part(line_of(k) * 2 + 1 - y).astype(BF16)
         for h in range(HALVES):
             pan_y(k, h).start()
 
-    def ms_onward(k, line):
+    def ms_own_parts(k):
+        parts = [ms_part(line_of(k + i) * 2 + y) for i in range(2)]
+        for i, part in enumerate(parts):
+            ms_total[i] = part
+
+    def ms_onward(k, i):
+        line = line_of(k)
         inner, row, slot = route(line)
-        ms_total[...] = ms_part(line * 2 + y)
         ms_y(k).wait_recv()
-        ms_total[...] += ms_y_recv[k].astype(F32)
+        ms_total[i] += ms_y_recv[k].astype(F32)
 
         @pl.when(inner)
         def _():
             ms_z(0, row, blocks + line).wait_recv()
-            ms_total[...] += ms_z_recv[blocks + line].astype(F32)
-
-        ms_z_send[k] = ms_total[...].astype(BF16)
+            ms_total[i] += ms_z_recv[blocks + line].astype(F32)
+
+        ms_z_send[k] = ms_total[i].astype(BF16)
         ms_z(k, row, slot).start()
 
-    def pan_onward(k, line):
+    def pan_onward(k):
+        line = line_of(k)
         inner, row, slot = route(line)
         pan_total[...] = pan_part(line * 2 + y)
         for h in range(HALVES):
@@ -391,57 +435,81 @@
             pan_z_send[k, rows] = pan_total[rows, :].astype(BF16)
             pan_z(k, h, row, slot).start()
 
-    each(0, lines, ms_to_twin)
-    each(0, 2, pan_to_twin)
-    each(0, lines - 1, ms_onward)
-    each(2, lines, pan_to_twin)
+    far = lines - 2
+
+    def ms_far_to_twin(p):
+        ms_to_twin(2 * p)
+        ms_y(2 * p).start()
+        ms_y(2 * p + 1).start()
+
+    def ms_far_onward(p):
+        ms_own_parts(2 * p)
+        ms_onward(2 * p, 0)
+        ms_onward(2 * p + 1, 1)
+
+    each(0, far // 2, ms_far_to_twin)
+    pan_to_twin(0)
+    ms_to_twin(far)
+    ms_y(far).start()
+    each(1, far, pan_to_twin)
+    ms_y(far + 1).start()
+    each(0, far // 2, ms_far_onward)
+    each(far, lines, pan_to_twin)
+    each(0, far - 1, pan_onward)
+    ms_own_parts(far)
+    ms_onward(far, 0)
+    pan_onward(far - 1)
 
     spot = (iota((coarse_cols, TC), 1).astype(F32) - 1.5) * 0.25 + 2.0
     tap = iota((coarse_cols, TC), 0) + 2
     up_cols[0:coarse_cols, :] = cubic_weight(spot - tap.astype(F32)).astype(BF16)
-    tap = tap + jnp.where(c == 0, coarse_cols, -coarse_cols)
-    up_cols[coarse_cols : 2 * coarse_cols, :] = cubic_weight(spot - tap.astype(F32)).astype(BF16)
-
-    each(0, 1, pan_onward)
-
-    ms_total[...] = ms_part(m)
+    tap = iota((LANES, TC), 0) % 2 + jnp.where(c == 0, coarse_cols + 2, 0)
+    up_cols[coarse_cols : coarse_cols + LANES, :] = cubic_weight(spot - tap.astype(F32)).astype(BF16)
+
     ms_y(lines - 1).wait_recv()
-    ms_total[...] += ms_y_recv[lines - 1].astype(F32)
+    ms_total[1] += ms_y_recv[lines - 1].astype(F32)
 
     def ms_arrived(slot, carry):
         ms_z(0, m, slot).wait_recv()
-        ms_total[...] += ms_z_recv[slot].astype(F32)
+        ms_total[1] += ms_z_recv[slot].astype(F32)
         return carry
 
     lax.fori_loop(0, blocks, ms_arrived, 0)
-    values = [ms_total[:, b * coarse_cols : (b + 1) * coarse_cols] for b in range(bands)]
+    for load in late_loads:
+        load.wait()
+    values = [ms_total[1, b * coarse_rows : (b + 1) * coarse_rows, :] for b in range(bands)]
     synthetic = sum(synth_ref[b] * values[b] for b in range(bands))
+    spot = iota((coarse_rows, LANES), 1) // 2
+    edges = jnp.zeros((coarse_rows, LANES), F32)
     for b in range(bands):
         result = values[b] - gain_ref[b] * synthetic
         for k in range(bands):
             result = result + mix_ref[b, k] * values[k]
-        window[half:mid, b * coarse_cols : (b + 1) * coarse_cols] = result.astype(BF16)
+        window[b, half:mid, :] = result.astype(BF16)
+        moved = pltpu.roll(result, jnp.where(c == 0, 2 * b + 2, 2 * b), 1)
+        edges = jnp.where(spot == b, moved, edges)
+    edge_own[half:mid, :] = edges.astype(BF16)
 
     has_above, has_below = m > 0, m < n - 1
 
-    def halo_copy(k, src, rows, dst, start, row, col):
-        return remote(
-            window.at[pl.ds(src, rows)],
-            dst.at[pl.ds(start, rows)],
-            halo_ss.at[k],
-            halo_rs.at[k],
-            row,
-            col,
-        )
-
-    across_copy = halo_copy(0, half, coarse_rows, beside, half, m, other)
-    up_copies = [
-        halo_copy(1, half, half, window, mid, m - 1, c),
-        halo_copy(2, half, half, beside, mid, m - 1, other),
-    ]
+    def halo_copy(k, src, dst, row, col):
+        return remote(src, dst, halo_ss.at[k], halo_rs.at[k], row, col)
+
+    def rows_copy(k, src, dst, row):
+        return halo_copy(
+            k, window.at[:, pl.ds(src, half)], window.at[:, pl.ds(dst, half)], row, c
+        )
+
+    def edge_copy(k, src, dst, rows, row):
+        return halo_copy(
+            k, edge_own.at[pl.ds(src, rows)], edge_all.at[pl.ds(dst, rows)], row, other
+        )
+
+    across_copy = edge_copy(0, half, half, coarse_rows, m)
+    up_copies = [rows_copy(1, half, mid, m - 1), edge_copy(2, half, mid, half, m - 1)]
     down_copies = [
-        halo_copy(3, coarse_rows, half, window, 0, m + 1, c),
-        halo_copy(4, coarse_rows, half, beside, 0, m + 1, other),
+        rows_copy(3, coarse_rows, 0, m + 1),
+        edge_copy(4, coarse_rows, 0, half, m + 1),
     ]
     across_copy.start()
 
@@ -455,7 +523,7 @@
         for copy in down_copies:
             copy.start()
 
-    each(1, lines - 1, pan_onward)
+    pan_onward(far)
     pan_total[...] = pan_part(m)
     across_copy.wait()
 
@@ -473,24 +541,43 @@
         for copy in up_copies:
             copy.wait_recv()
 
-    edge = jnp.zeros((half, window.shape[1]), BF16)
+    blank = jnp.zeros((bands, half, coarse_cols), BF16)
+    blank_edge = jnp.zeros((half, LANES), BF16)
 
     @pl.when(jnp.logical_not(has_above))
     def _():
-        window[0:half, :] = edge
-        beside[0:half, :] = edge
+        window[:, 0:half, :] = blank
+        edge_all[0:half, :] = blank_edge
 
     @pl.when(jnp.logical_not(has_below))
     def _():
-        window[mid : mid + half, :] = edge
-        beside[mid : mid + half, :] = edge
-
-    for b in range(bands):
-        lanes = slice(b * coarse_cols, (b + 1) * coarse_cols)
-        source = jnp.concatenate([window[:, lanes], beside[:, lanes]], axis=1)
-        across = jnp.dot(source, up_cols[...], preferred_element_type=F32)
-        mixed[b] = jnp.dot(up_rows[...], across.astype(BF16), preferred_element_type=F32)
-
+        window[:, mid : mid + half, :] = blank
+        edge_all[mid : mid + half, :] = blank_edge
+
+    edges = edge_all[...]
+    spot = iota(edges.shape, 1) // 2
+    for first in range(0, bands, GROUP):
+        group = range(first, min(first + GROUP, bands))
+        source = jnp.concatenate(
+            [
+                jnp.concatenate(
+                    [window[b], jnp.where(spot == b, edges, jnp.zeros_like(edges))], axis=1
+                )
+                for b in group
+            ],
+            axis=0,
+        )
+        across = jnp.dot(source, up_cols[...], preferred_element_type=F32).astype(BF16)
+        for b in group:
+            begin = (b - first) * 2 * coarse_rows
+            mixed[b] = jnp.dot(
+                up_rows[...],
+                across[begin : begin + 2 * coarse_rows, :],
+                preferred_element_type=F32,
+            ).astype(BF16)
+
+    store = pltpu.make_async_copy(mixed, mixed_hbm, load_sem.at[9])
+    store.start()
     for h in range(HALVES):
         rows = slice(h * part_rows, (h + 1) * part_rows)
         pan_y(lines - 1, h).wait_recv()
@@ -502,10 +589,6 @@
             return carry
 
         lax.fori_loop(0, blocks, pan_arrived, 0)
-        for b in range(bands):
-            out_ref[b, rows, :] = (mixed[b, rows, :] + gain_ref[b] * pan_total[rows, :]).astype(
-                BF16
-            )
 
     def y_sent(k, carry):
         ms_y(k).wait_send()
@@ -521,6 +604,7 @@
 
     lax.fori_loop(0, lines, y_sent, 0)
     lax.fori_loop(0, lines - 1, z_sent, 0)
+    store.wait()
 
 
 def local(
@@ -541,26 +625,33 @@
     capacity = tile_list.shape[1] // n
     bands = band_gain.shape[0]
     coarse_rows, coarse_cols = TR // 4, TC // 4
-    ms_width = bands * coarse_cols
     table_rows = pl.cdiv(2 + pl.cdiv(n * KR * KC, LANES), 8) * 8
-    smem = pl.BlockSpec(memory_space=pltpu.SMEM)
     vmem = pl.BlockSpec(memory_space=pltpu.VMEM)
     hbm = pl.BlockSpec(memory_space=pl.ANY)
     dma = pltpu.SemaphoreType.DMA
     slots = lines // 2 + lines
 
     def ms_slots(count):
-        return pltpu.VMEM((count, coarse_rows, ms_width), BF16)
+        return pltpu.VMEM((count, bands * coarse_rows, coarse_cols), BF16)
 
     def pan_slots(count):
         return pltpu.VMEM((count, TR, TC), BF16)
 
-    return pl.pallas_call(
+    mixed, pan_map = pl.pallas_call(
         functools.partial(mapping, capacity, col_grid.shape[1]),
-        out_shape=jax.ShapeDtypeStruct((bands, TR, TC), BF16),
-        in_specs=[vmem, vmem, vmem, hbm, hbm, smem, smem, smem],
-        out_specs=vmem,
+        out_shape=(
+            jax.ShapeDtypeStruct((bands, TR, TC), BF16),
+            jax.ShapeDtypeStruct((TR, TC), F32),
+        ),
+        in_specs=[hbm] * 8,
+        out_specs=(hbm, vmem),
         scratch_shapes=[
+            pltpu.VMEM(send_list.shape, I32),
+            pltpu.VMEM((1, row_grid.shape[0]), F32),
+            pltpu.VMEM(col_grid.shape, F32),
+            pltpu.SMEM(band_mix.shape, F32),
+            pltpu.SMEM(band_gain.shape, F32),
+            pltpu.SMEM(synth_weight.shape, F32),
             pltpu.VMEM(pan_blocks.shape, BF16),
             pltpu.VMEM(ms_blocks.shape, BF16),
             pltpu.VMEM((own_blocks + 1, size, size), BF16),
@@ -577,16 +668,14 @@
             ms_slots(slots),
             pan_slots(lines - 1),
             pan_slots(slots),
-            pltpu.VMEM((coarse_rows, ms_width), F32),
-            pltpu.VMEM((TR, TC), F32),
-            pltpu.VMEM((KC * size, TC), BF16),
-            pltpu.VMEM((KC * bands * coarse_size, ms_width), BF16),
-            pltpu.VMEM((2 * coarse_rows, ms_width), BF16),
-            pltpu.VMEM((2 * coarse_rows, ms_width), BF16),
-            pltpu.VMEM((2 * coarse_cols, TC), BF16),
+            pltpu.VMEM((2, bands * coarse_rows, coarse_cols), F32),
+            pltpu.VMEM((bands, 2 * coarse_rows, coarse_cols), BF16),
+            pltpu.VMEM((2 * coarse_rows, LANES), BF16),
+            pltpu.VMEM((2 * coarse_rows, LANES), BF16),
+            pltpu.VMEM((coarse_cols + LANES, TC), BF16),
             pltpu.VMEM((TR, 2 * coarse_rows), BF16),
-            pltpu.VMEM((bands, TR, TC), F32),
-            dma((3,)),
+            pltpu.VMEM((bands, TR, TC), BF16),
+            dma((10,)),
             dma((2, n)),
             dma((2, n)),
             dma((lines,)),
@@ -601,7 +690,7 @@
             dma((5,)),
         ],
         compiler_params=pltpu.CompilerParams(
-            collective_id=0, has_side_effects=True, vmem_limit_bytes=40 * 1024 * 1024
+            collective_id=0, has_side_effects=True, vmem_limit_bytes=60 * 1024 * 1024
         ),
         name="mapping",
     )(
@@ -614,6 +703,8 @@
         band_gain,
         synth_weight,
     )
+    detail = band_gain[:, None, None] * pan_map[None]
+    return (mixed.astype(F32) + detail).astype(BF16)
 
 
 def solution(mesh):

time: 45 us -> 35.8 us (0.80)
  local copies, waits for them, and re-layouts: 7.77 us -> 0.01 us
  Pallas kernels: 36.8 us -> 33 us
  other arithmetic: 0 us -> 2.61 us
    unnamed x17 -> x2, local copies, waits for them, and re-layouts: 7.77 us -> 0.01 us
    pallas_call x1, Pallas kernels: 36.8 us -> 33 us  [local(): pl.pallas_call(functools.partial(mapping, capacity, col_grid.shape[1]), o...]
    convert_element_type x0 -> x1, other arithmetic: none -> 2.61 us  [local(): return (mixed.astype(F32) + detail).astype(BF16)]
where the time goes in v2:
time: 35.8 us; the launch traced here: 35.6 us
  Pallas kernels  33 us (92%)
  other arithmetic  2.61 us (7%)
    pallas_call x1, Pallas kernels, local(): pl.pallas_call(functools.partial(mapping, capacity, col_grid.shape[1]), o...  33 us
    convert_element_type x1, other arithmetic, local(): return (mixed.astype(F32) + detail).astype(BF16)  2.61 us

profile of v2, /device:TPU:0, one launch (start us, length us, event | category | flops | bytes accessed | tf_op | source)
XLA Modules:
  0.0 35.6 jit_solution(17637157526194563895)
XLA Ops:
  0.0 0.0 copy-start
  0.0 33.0 %mapping.1 = (bf16[8,128,512]{2,1,0:T(8,128)(2,1)}, f32[128,512]{1,0:T(8,128)}) custom-call(s32[3,64]{1,0:T(4,128)} %send_hbm.1, f32[1,3]{1,0:T(1,128)} %bitcast.1, f32[1,8]{1,0:T(1,128)} %col_hbm.1, bf16[64,128,128]{2,1,0:T(8,128)(2,1)} %pan_hbm.1, bf16[64,32,256]{2,1,0:T(8,128)(2,1)} %ms_hbm.1, f32[8,8]{1,0:T(8,128)} %mix_hbm.1, f32[8]{0:T(128)} %gain_hbm.1, ...), custom_call_target="tpu_custom_call" | custom-call | tf_op jit(solution)/shard_map/mapping/pallas_call | solution.py:640
  33.0 0.0 copy-done
  33.0 2.6 %add_convert_fusion = bf16[8,128,512]{2,1,0:T(8,128)(2,1)} fusion(bf16[8,128,512]{2,1,0:T(8,128)(2,1)} %get-tuple-element.7, f32[128,512]{1,0:T(8,128)} %get-tuple-element.8, f32[8]{0:T(128)S(1)} %copy-done), kind=kLoop, calls=%fused_computation | loop fusion | flops 2097152 | bytes 2359328 | tf_op jit(solution)/shard_map/convert_element_type | solution.py:707
Async XLA Ops:
  0.0 33.0 %copy-start = (f32[8]{0:T(128)S(1)}, f32[8]{0:T(128)}, u32[]{:S(2)}) copy-start(f32[8]{0:T(128)} %gain_hbm.1) | copy-start | bytes 100

commit v3 on v2

--- a/solution.py
+++ b/solution.py
@@ -15,7 +15,6 @@
 LANES = 128
 PACK = 16
 HALVES = 2
-GROUP = 4
 MESH = pl.DeviceIdType.MESH
 F32 = jnp.float32
 BF16 = jnp.bfloat16
@@ -35,8 +34,8 @@
 
 def row_coord(nodes, position, offset):
     first = position < GRID
-    a = jnp.where(first, nodes[0:1, 0:1], nodes[0:1, 1:2])
-    b = jnp.where(first, nodes[0:1, 1:2], nodes[0:1, 2:3])
+    a = jnp.where(first, nodes[:, 0:1], nodes[:, 1:2])
+    b = jnp.where(first, nodes[:, 1:2], nodes[:, 2:3])
     within = (jnp.where(first, position, position - GRID).astype(F32) + offset) / GRID
     return a + (b - a) * within
 
@@ -45,12 +44,12 @@
     segment = position // GRID
     coord = jnp.zeros(position.shape, F32)
     for s in range(count):
-        left, shift = nodes[1:2, s : s + 1], s * GRID
+        left, shift = nodes[:, s : s + 1], s * GRID
         if s + 1 < count:
-            right = nodes[1:2, s + 1 : s + 2]
+            right = nodes[:, s + 1 : s + 2]
         else:
             right = jnp.where(is_last, left, after)
-            left = jnp.where(is_last, nodes[1:2, s - 1 : s], left)
+            left = jnp.where(is_last, nodes[:, s - 1 : s], left)
             shift = jnp.where(is_last, shift - GRID, shift)
         within = ((position - shift).astype(F32) + offset) / GRID
         coord = jnp.where(segment == s, left + (right - left) * within, coord)
@@ -95,8 +94,6 @@
     mixed_hbm,
     pan_total,
     send_ref,
-    row_ref,
-    col_ref,
     mix_ref,
     gain_ref,
     synth_ref,
@@ -106,8 +103,8 @@
     ms_sum,
     table_ref,
     table,
-    nodes_ref,
-    nodes_all,
+    rows_all,
+    cols_all,
     ms_y_send,
     ms_y_recv,
     pan_y_send,
@@ -116,16 +113,30 @@
     ms_z_recv,
     pan_z_send,
     pan_z_recv,
+    near_ms_send,
+    near_ms_recv,
+    near_pan_send,
+    near_pan_recv,
     ms_total,
+    ms_hold,
+    pan_part_sum,
+    pan_hold,
     window,
+    rim_send,
+    rim_recv,
+    edge_send,
+    edge_recv,
     edge_own,
     edge_all,
     up_cols,
     up_rows,
+    across,
     mixed,
     load_sem,
-    nodes_ss,
-    nodes_rs,
+    rows_ss,
+    rows_rs,
+    cols_ss,
+    cols_rs,
     ms_y_ss,
     ms_y_rs,
     pan_y_ss,
@@ -134,6 +145,8 @@
     ms_z_rs,
     pan_z_ss,
     pan_z_rs,
+    near_ss,
+    near_rs,
     halo_ss,
     halo_rs,
 ):
@@ -154,8 +167,6 @@
     bands = mixed.shape[0]
     coarse_rows = TR // 4
     coarse_cols = TC // 4
-    half = coarse_rows // 2
-    mid = half + coarse_rows
     part_rows = TR // HALVES
     first_col = c * KC
     is_last = c == lax.axis_size("mcol") - 1
@@ -187,8 +198,8 @@
         pltpu.make_async_copy(src, dst, load_sem.at[k])
         for k, (src, dst) in enumerate(
             (
-                (row_hbm, row_ref),
-                (col_hbm, col_ref),
+                (row_hbm, rows_all.at[m]),
+                (col_hbm, cols_all.at[c, m]),
                 (send_hbm, send_ref),
                 (ms_hbm, ms_ref),
                 (pan_hbm, pan_ref),
@@ -202,32 +213,30 @@
         load.start()
     row_load, col_load, send_load, ms_load, pan_load, *late_loads = loads
 
-    nodes_ref[...] = jnp.zeros_like(nodes_ref)
-    row_load.wait()
-    col_load.wait()
-    nodes_ref[0:1, 0 : row_ref.shape[1]] = row_ref[...]
-    nodes_ref[1:2, 0 : col_ref.shape[1]] = col_ref[...]
-    nodes_all[c, m] = nodes_ref[...]
     pl.semaphore_wait(barrier, 2 * n - 1)
 
-    def nodes_copy(slot_row, slot_col, row, col):
+    def rows_copy(slot, row):
+        return remote(row_hbm, rows_all.at[slot], rows_ss.at[row], rows_rs.at[slot], row, c)
+
+    def cols_copy(slot_row, slot_col, row, col):
         return remote(
-            nodes_ref,
-            nodes_all.at[slot_col, slot_row],
-            nodes_ss.at[col, row],
-            nodes_rs.at[slot_col, slot_row],
+            col_hbm,
+            cols_all.at[slot_col, slot_row],
+            cols_ss.at[col, row],
+            cols_rs.at[slot_col, slot_row],
             row,
             col,
         )
 
     def send_nodes(k, carry):
         row = lax.rem(m + k, n)
-        nodes_copy(m, c, row, c).start()
-        nodes_copy(m, c, row, other).start()
+        cols_copy(m, c, row, other).start()
+        cols_copy(m, c, row, c).start()
+        rows_copy(m, row).start()
         return carry
 
     lax.fori_loop(1, n, send_nodes, 0)
-    nodes_copy(m, c, m, other).start()
+    cols_copy(m, c, m, other).start()
     send_load.wait()
 
     square = (own_blocks, own_blocks)
@@ -254,8 +263,12 @@
     table_copy = pltpu.make_async_copy(table_ref, table, load_sem.at[8])
     table_copy.start()
 
-    tap = iota((TR, 2 * coarse_rows), 1) - (half - 2)
-    spot = (iota((TR, 2 * coarse_rows), 0).astype(F32) - 1.5) * 0.25 + 2.0
+    column = iota(up_rows.shape, 1)
+    rim = column - coarse_rows
+    tap = jnp.where(
+        column < coarse_rows, column + 2, rim % 2 + jnp.where(rim < 2 * bands, 0, coarse_rows + 2)
+    )
+    spot = (iota(up_rows.shape, 0).astype(F32) - 1.5) * 0.25 + 2.0
     up_rows[...] = cubic_weight(spot - tap.astype(F32)).astype(BF16)
     pan_sum[0] = jnp.zeros((size, size), BF16)
     ms_sum[0] = jnp.zeros((coarse_size, coarse_width), BF16)
@@ -277,12 +290,15 @@
 
     def wait_nodes(k, carry):
         row = lax.rem(m + k, n)
-        nodes_copy(row, c, row, c).wait()
-        nodes_copy(row, other, row, other).wait()
+        cols_copy(row, c, row, c).wait()
+        cols_copy(row, other, row, other).wait()
+        rows_copy(row, row).wait()
         return carry
 
+    row_load.wait()
+    col_load.wait()
     lax.fori_loop(1, n, wait_nodes, 0)
-    nodes_copy(m, other, m, other).wait()
+    cols_copy(m, other, m, other).wait()
 
     def cell_of(sums, tile, row, col):
         cell = (tile * KR + row) * KC + col
@@ -292,14 +308,14 @@
         return jnp.concatenate([cell_of(sums, tile, row, col) for row in range(KR)], axis=0)
 
     def ms_part(tile):
-        nodes = nodes_all[c, tile]
-        after = nodes_all[1, tile][1:2, 0:1]
+        row_nodes, nodes = rows_all[tile], cols_all[c, tile]
+        after = cols_all[1, tile][:, 0:1]
         x_ms = col_coord(
             nodes, after, is_last, col_nodes, 4 * iota((1, coarse_cols), 1) + 1, 0.5
         )
         x_ms = (x_ms - 1.5) * 0.25
         col = spread(x_ms, (first_col * coarse_size).astype(F32), KC * coarse_size)
-        spots = (row_coord(nodes, 4 * iota((coarse_rows, 1), 0) + 1, 0.5) - 1.5) * 0.25
+        spots = (row_coord(row_nodes, 4 * iota((coarse_rows, 1), 0) + 1, 0.5) - 1.5) * 0.25
         taps = iota((coarse_rows, KR * coarse_size), 1).astype(F32)
         weight = cubic_weight(spots - taps).astype(BF16)
         rows = [
@@ -315,11 +331,11 @@
         return jnp.dot(jnp.concatenate(by_band, axis=0), col, preferred_element_type=F32)
 
     def pan_part(tile):
-        nodes = nodes_all[c, tile]
-        after = nodes_all[1, tile][1:2, 0:1]
+        row_nodes, nodes = rows_all[tile], cols_all[c, tile]
+        after = cols_all[1, tile][:, 0:1]
         x_pan = col_coord(nodes, after, is_last, col_nodes, iota((1, TC), 1), 0.0)
         col = spread(x_pan, (first_col * size).astype(F32), KC * size)
-        row = spread(row_coord(nodes, iota((1, TR), 1), 0.0), 0.0, KR * size)
+        row = spread(row_coord(row_nodes, iota((1, TR), 1), 0.0), 0.0, KR * size)
         rows = []
         for k in range(0, KC, 2):
             source = jnp.concatenate(
@@ -389,13 +405,23 @@
 
         lax.fori_loop(first, last, body, 0)
 
-    def ms_to_twin(k):
-        parts = [ms_part(line_of(k + i) * 2 + 1 - y) for i in range(2)]
-        for i, part in enumerate(parts):
-            ms_y_send[k + i] = part.astype(BF16)
+    near_row = partner * 2 + y
+
+    def near(k, src, dst):
+        return remote(src, dst, near_ss.at[k], near_rs.at[k], near_row, c)
+
+    near_ms = near(0, near_ms_send, near_ms_recv)
+    near_pan = near(1, near_pan_send, near_pan_recv)
+    first_rows = slice(0, part_rows)
+
+    def ms_twin_parts(k):
+        return [ms_part(line_of(k + i) * 2 + 1 - y) for i in range(2)]
+
+    def pan_twin_part(k):
+        return pan_part(line_of(k) * 2 + 1 - y)
 
     def pan_to_twin(k):
-        pan_y_send[k] = pan_part(line_of(k) * 2 + 1 - y).astype(BF16)
+        pan_y_send[k] = pan_twin_part(k).astype(BF16)
         for h in range(HALVES):
             pan_y(k, h).start()
 
@@ -421,24 +447,26 @@
     def pan_onward(k):
         line = line_of(k)
         inner, row, slot = route(line)
-        pan_total[...] = pan_part(line * 2 + y)
+        pan_part_sum[...] = pan_part(line * 2 + y)
         for h in range(HALVES):
             rows = slice(h * part_rows, (h + 1) * part_rows)
             pan_y(k, h).wait_recv()
-            pan_total[rows, :] += pan_y_recv[k, rows].astype(F32)
+            pan_part_sum[rows, :] += pan_y_recv[k, rows].astype(F32)
 
             @pl.when(inner)
             def _():
                 pan_z(0, h, row, blocks + line).wait_recv()
-                pan_total[rows, :] += pan_z_recv[blocks + line, rows].astype(F32)
-
-            pan_z_send[k, rows] = pan_total[rows, :].astype(BF16)
+                pan_part_sum[rows, :] += pan_z_recv[blocks + line, rows].astype(F32)
+
+            pan_z_send[k, rows] = pan_part_sum[rows, :].astype(BF16)
             pan_z(k, h, row, slot).start()
 
     far = lines - 2
+    last = lines - 1
 
     def ms_far_to_twin(p):
-        ms_to_twin(2 * p)
+        for i, part in enumerate(ms_twin_parts(2 * p)):
+            ms_y_send[2 * p + i] = part.astype(BF16)
         ms_y(2 * p).start()
         ms_y(2 * p + 1).start()
 
@@ -448,17 +476,41 @@
         ms_onward(2 * p + 1, 1)
 
     each(0, far // 2, ms_far_to_twin)
+    parts = ms_twin_parts(far)
+    near_ms_send[...] = parts[0].astype(BF16)
+    ms_hold[...] = parts[1]
+    near_ms.start()
     pan_to_twin(0)
-    ms_to_twin(far)
-    ms_y(far).start()
+    pan_y_send[far] = pan_twin_part(far).astype(BF16)
+    near_pan_send[...] = pan_y_send[far, first_rows]
+    near_pan.start()
     each(1, far, pan_to_twin)
-    ms_y(far + 1).start()
+    for h in range(1, HALVES):
+        pan_y(far, h).start()
+    pan_hold[...] = pan_twin_part(last)
+    near_ms.wait_recv()
+    ms_y_send[last] = (ms_hold[...] + near_ms_recv[...].astype(F32)).astype(BF16)
+    ms_y(last).start()
+    near_pan.wait_recv()
+    pan_hold[first_rows, :] += near_pan_recv[...].astype(F32)
+    pan_y_send[last] = pan_hold[...].astype(BF16)
+    for h in range(HALVES):
+        pan_y(last, h).start()
     each(0, far // 2, ms_far_onward)
-    each(far, lines, pan_to_twin)
-    each(0, far - 1, pan_onward)
+
+    early = route(line_of(far - 1))[0]
     ms_own_parts(far)
-    ms_onward(far, 0)
-    pan_onward(far - 1)
+    ms_z_send[far] = ms_total[0].astype(BF16)
+    pan_hold[...] = pan_part(near_row)
+    pan_z_send[far, first_rows] = pan_hold[first_rows, :].astype(BF16)
+
+    def near_start():
+        ms_z(far, near_row, pair).start()
+        pan_z(far, 0, near_row, pair).start()
+
+    pl.when(early)(near_start)
+    each(0, far, pan_onward)
+    pl.when(jnp.logical_not(early))(near_start)
 
     spot = (iota((coarse_cols, TC), 1).astype(F32) - 1.5) * 0.25 + 2.0
     tap = iota((coarse_cols, TC), 0) + 2
@@ -466,8 +518,8 @@
     tap = iota((LANES, TC), 0) % 2 + jnp.where(c == 0, coarse_cols + 2, 0)
     up_cols[coarse_cols : coarse_cols + LANES, :] = cubic_weight(spot - tap.astype(F32)).astype(BF16)
 
-    ms_y(lines - 1).wait_recv()
-    ms_total[1] += ms_y_recv[lines - 1].astype(F32)
+    ms_y(last).wait_recv()
+    ms_total[1] += ms_y_recv[last].astype(F32)
 
     def ms_arrived(slot, carry):
         ms_z(0, m, slot).wait_recv()
@@ -481,35 +533,36 @@
     synthetic = sum(synth_ref[b] * values[b] for b in range(bands))
     spot = iota((coarse_rows, LANES), 1) // 2
     edges = jnp.zeros((coarse_rows, LANES), F32)
+    tops, bottoms = [], []
     for b in range(bands):
         result = values[b] - gain_ref[b] * synthetic
         for k in range(bands):
             result = result + mix_ref[b, k] * values[k]
-        window[b, half:mid, :] = result.astype(BF16)
+        window[b] = result.astype(BF16)
         moved = pltpu.roll(result, jnp.where(c == 0, 2 * b + 2, 2 * b), 1)
         edges = jnp.where(spot == b, moved, edges)
-    edge_own[half:mid, :] = edges.astype(BF16)
+        tops.append(result[0:2, :])
+        bottoms.append(result[coarse_rows - 2 : coarse_rows, :])
+    edge_own[...] = edges.astype(BF16)
+    rim_send[0] = jnp.concatenate(tops, axis=0).astype(BF16)
+    rim_send[1] = jnp.concatenate(bottoms, axis=0).astype(BF16)
+    edge_send[0] = jnp.concatenate([edges[0:2, :]] * bands, axis=0).astype(BF16)
+    bottom = edges[coarse_rows - 2 : coarse_rows, :]
+    edge_send[1] = jnp.concatenate([bottom] * bands, axis=0).astype(BF16)
 
     has_above, has_below = m > 0, m < n - 1
 
     def halo_copy(k, src, dst, row, col):
         return remote(src, dst, halo_ss.at[k], halo_rs.at[k], row, col)
 
-    def rows_copy(k, src, dst, row):
-        return halo_copy(
-            k, window.at[:, pl.ds(src, half)], window.at[:, pl.ds(dst, half)], row, c
-        )
-
-    def edge_copy(k, src, dst, rows, row):
-        return halo_copy(
-            k, edge_own.at[pl.ds(src, rows)], edge_all.at[pl.ds(dst, rows)], row, other
-        )
-
-    across_copy = edge_copy(0, half, half, coarse_rows, m)
-    up_copies = [rows_copy(1, half, mid, m - 1), edge_copy(2, half, mid, half, m - 1)]
+    across_copy = halo_copy(0, edge_own, edge_all, m, other)
+    up_copies = [
+        halo_copy(1, rim_send.at[0], rim_recv.at[1], m - 1, c),
+        halo_copy(2, edge_send.at[0], edge_recv.at[1], m - 1, other),
+    ]
     down_copies = [
-        rows_copy(3, coarse_rows, 0, m + 1),
-        edge_copy(4, coarse_rows, 0, half, m + 1),
+        halo_copy(3, rim_send.at[1], rim_recv.at[0], m + 1, c),
+        halo_copy(4, edge_send.at[1], edge_recv.at[0], m + 1, other),
     ]
     across_copy.start()
 
@@ -523,9 +576,36 @@
         for copy in down_copies:
             copy.start()
 
-    pan_onward(far)
+    for h in range(1, HALVES):
+        rows = slice(h * part_rows, (h + 1) * part_rows)
+        pan_y(far, h).wait_recv()
+        pan_hold[rows, :] += pan_y_recv[far, rows].astype(F32)
+        pan_z_send[far, rows] = pan_hold[rows, :].astype(BF16)
+        pan_z(far, h, near_row, pair).start()
     pan_total[...] = pan_part(m)
     across_copy.wait()
+
+    edges = edge_all[...]
+    spot = iota(edges.shape, 1) // 2
+    source = jnp.concatenate(
+        [
+            jnp.concatenate(
+                [window[b], jnp.where(spot == b, edges, jnp.zeros_like(edges))], axis=1
+            )
+            for b in range(bands)
+        ],
+        axis=0,
+    )
+    across[0 : bands * coarse_rows, :] = jnp.dot(
+        source, up_cols[...], preferred_element_type=F32
+    ).astype(BF16)
+    for b in range(bands):
+        own = slice(b * coarse_rows, (b + 1) * coarse_rows)
+        mixed[b, PACK : TR - PACK, :] = jnp.dot(
+            up_rows[PACK : TR - PACK, 0:coarse_rows],
+            across[own, :],
+            preferred_element_type=F32,
+        ).astype(BF16)
 
     @pl.when(has_above)
     def _():
@@ -541,47 +621,46 @@
         for copy in up_copies:
             copy.wait_recv()
 
-    blank = jnp.zeros((bands, half, coarse_cols), BF16)
-    blank_edge = jnp.zeros((half, LANES), BF16)
+    blank = jnp.zeros((2 * bands, LANES), BF16)
 
     @pl.when(jnp.logical_not(has_above))
     def _():
-        window[:, 0:half, :] = blank
-        edge_all[0:half, :] = blank_edge
+        rim_recv[0] = blank
+        edge_recv[0] = blank
 
     @pl.when(jnp.logical_not(has_below))
     def _():
-        window[:, mid : mid + half, :] = blank
-        edge_all[mid : mid + half, :] = blank_edge
-
-    edges = edge_all[...]
-    spot = iota(edges.shape, 1) // 2
-    for first in range(0, bands, GROUP):
-        group = range(first, min(first + GROUP, bands))
-        source = jnp.concatenate(
-            [
-                jnp.concatenate(
-                    [window[b], jnp.where(spot == b, edges, jnp.zeros_like(edges))], axis=1
-                )
-                for b in group
-            ],
-            axis=0,
-        )
-        across = jnp.dot(source, up_cols[...], preferred_element_type=F32).astype(BF16)
-        for b in group:
-            begin = (b - first) * 2 * coarse_rows
-            mixed[b] = jnp.dot(
-                up_rows[...],
-                across[begin : begin + 2 * coarse_rows, :],
-                preferred_element_type=F32,
-            ).astype(BF16)
+        rim_recv[1] = blank
+        edge_recv[1] = blank
+
+    spot = iota((2 * bands, LANES), 1) // 2
+    mine = spot == iota((2 * bands, LANES), 0) // 2
+    source = jnp.concatenate(
+        [
+            jnp.concatenate([rim_recv[i], jnp.where(mine, edge_recv[i], blank)], axis=1)
+            for i in range(2)
+        ],
+        axis=0,
+    )
+    rims = jnp.dot(source, up_cols[...], preferred_element_type=F32).astype(BF16)
+    outer = jnp.concatenate([up_rows[0:PACK, :], up_rows[TR - PACK : TR, :]], axis=0)
+    column = iota(outer.shape, 1)
+    owner_band = (column - coarse_rows) % (2 * bands) // 2
+    for b in range(bands):
+        weight = jnp.where((column < coarse_rows) | (owner_band == b), outer, jnp.zeros_like(outer))
+        own = slice(b * coarse_rows, (b + 1) * coarse_rows)
+        ends = jnp.dot(
+            weight, jnp.concatenate([across[own, :], rims], axis=0), preferred_element_type=F32
+        ).astype(BF16)
+        mixed[b, 0:PACK, :] = ends[0:PACK, :]
+        mixed[b, TR - PACK : TR, :] = ends[PACK : 2 * PACK, :]
 
     store = pltpu.make_async_copy(mixed, mixed_hbm, load_sem.at[9])
     store.start()
     for h in range(HALVES):
         rows = slice(h * part_rows, (h + 1) * part_rows)
-        pan_y(lines - 1, h).wait_recv()
-        pan_total[rows, :] += pan_y_recv[lines - 1, rows].astype(F32)
+        pan_y(last, h).wait_recv()
+        pan_total[rows, :] += pan_y_recv[last, rows].astype(F32)
 
         def pan_arrived(slot, carry):
             pan_z(0, h, m, slot).wait_recv()
@@ -592,7 +671,11 @@
 
     def y_sent(k, carry):
         ms_y(k).wait_send()
-        for h in range(HALVES):
+        pan_y(k, 0).wait_send()
+        return carry
+
+    def y_rest_sent(k, carry):
+        for h in range(1, HALVES):
             pan_y(k, h).wait_send()
         return carry
 
@@ -602,7 +685,11 @@
             pan_z(k, h, m, 0).wait_send()
         return carry
 
-    lax.fori_loop(0, lines, y_sent, 0)
+    near_ms.wait_send()
+    near_pan.wait_send()
+    lax.fori_loop(0, far, y_sent, 0)
+    lax.fori_loop(last, lines, y_sent, 0)
+    lax.fori_loop(0, lines, y_rest_sent, 0)
     lax.fori_loop(0, lines - 1, z_sent, 0)
     store.wait()
 
@@ -647,8 +734,6 @@
         out_specs=(hbm, vmem),
         scratch_shapes=[
             pltpu.VMEM(send_list.shape, I32),
-            pltpu.VMEM((1, row_grid.shape[0]), F32),
-            pltpu.VMEM(col_grid.shape, F32),
             pltpu.SMEM(band_mix.shape, F32),
             pltpu.SMEM(band_gain.shape, F32),
             pltpu.SMEM(synth_weight.shape, F32),
@@ -658,8 +743,8 @@
             pltpu.VMEM((own_blocks + 1, coarse_size, coarse_width), BF16),
             pltpu.VMEM((table_rows, LANES), I32),
             pltpu.SMEM((table_rows, LANES), I32),
-            pltpu.VMEM((8, LANES), F32),
-            pltpu.VMEM((2, n, 8, LANES), F32),
+            pltpu.VMEM((n, 1, row_grid.shape[0]), F32),
+            pltpu.VMEM((2, n) + col_grid.shape, F32),
             ms_slots(lines),
             ms_slots(lines),
             pan_slots(lines),
@@ -668,14 +753,28 @@
             ms_slots(slots),
             pan_slots(lines - 1),
             pan_slots(slots),
+            pltpu.VMEM((bands * coarse_rows, coarse_cols), BF16),
+            pltpu.VMEM((bands * coarse_rows, coarse_cols), BF16),
+            pltpu.VMEM((TR // HALVES, TC), BF16),
+            pltpu.VMEM((TR // HALVES, TC), BF16),
             pltpu.VMEM((2, bands * coarse_rows, coarse_cols), F32),
-            pltpu.VMEM((bands, 2 * coarse_rows, coarse_cols), BF16),
-            pltpu.VMEM((2 * coarse_rows, LANES), BF16),
-            pltpu.VMEM((2 * coarse_rows, LANES), BF16),
+            pltpu.VMEM((bands * coarse_rows, coarse_cols), F32),
+            pltpu.VMEM((TR, TC), F32),
+            pltpu.VMEM((TR, TC), F32),
+            pltpu.VMEM((bands, coarse_rows, coarse_cols), BF16),
+            pltpu.VMEM((2, 2 * bands, LANES), BF16),
+            pltpu.VMEM((2, 2 * bands, LANES), BF16),
+            pltpu.VMEM((2, 2 * bands, LANES), BF16),
+            pltpu.VMEM((2, 2 * bands, LANES), BF16),
+            pltpu.VMEM((coarse_rows, LANES), BF16),
+            pltpu.VMEM((coarse_rows, LANES), BF16),
             pltpu.VMEM((coarse_cols + LANES, TC), BF16),
-            pltpu.VMEM((TR, 2 * coarse_rows), BF16),
+            pltpu.VMEM((TR, coarse_rows + 4 * bands), BF16),
+            pltpu.VMEM((bands * coarse_rows, TC), BF16),
             pltpu.VMEM((bands, TR, TC), BF16),
             dma((10,)),
+            dma((n,)),
+            dma((n,)),
             dma((2, n)),
             dma((2, n)),
             dma((lines,)),
@@ -686,6 +785,8 @@
             dma((slots,)),
             dma((lines - 1, HALVES)),
             dma((slots, HALVES)),
+            dma((2,)),
+            dma((2,)),
             dma((5,)),
             dma((5,)),
         ],

time: 35.8 us -> 36.3 us (1.014)
  Pallas kernels: 33 us -> 33.5 us
    pallas_call x1, Pallas kernels: 33 us -> 33.5 us  [local(): pl.pallas_call(functools.partial(mapping, capacity, col_grid.shape[1]), o...]
where the time goes in v3:
time: 36.3 us; the launch traced here: 36.1 us
  Pallas kernels  33.5 us (92%)
  other arithmetic  2.61 us (7%)
    pallas_call x1, Pallas kernels, local(): pl.pallas_call(functools.partial(mapping, capacity, col_grid.shape[1]), o...  33.5 us
    convert_element_type x1, other arithmetic, local(): return (mixed.astype(F32) + detail).astype(BF16)  2.61 us

profile of v3, /device:TPU:0, one launch (start us, length us, event | category | flops | bytes accessed | tf_op | source)
XLA Modules:
  0.0 36.1 jit_solution(11875320390009266683)
XLA Ops:
  0.0 0.0 copy-start
  0.0 33.5 %mapping.1 = (bf16[8,128,512]{2,1,0:T(8,128)(2,1)}, f32[128,512]{1,0:T(8,128)}) custom-call(s32[3,64]{1,0:T(4,128)} %send_hbm.1, f32[1,3]{1,0:T(1,128)} %bitcast.1, f32[1,8]{1,0:T(1,128)} %col_hbm.1, bf16[64,128,128]{2,1,0:T(8,128)(2,1)} %pan_hbm.1, bf16[64,32,256]{2,1,0:T(8,128)(2,1)} %ms_hbm.1, f32[8,8]{1,0:T(8,128)} %mix_hbm.1, f32[8]{0:T(128)} %gain_hbm.1, ...), custom_call_target="tpu_custom_call" | custom-call | tf_op jit(solution)/shard_map/mapping/pallas_call | solution.py:727
  33.5 0.0 copy-done
  33.5 2.6 %add_convert_fusion = bf16[8,128,512]{2,1,0:T(8,128)(2,1)} fusion(bf16[8,128,512]{2,1,0:T(8,128)(2,1)} %get-tuple-element.7, f32[128,512]{1,0:T(8,128)} %get-tuple-element.8, f32[8]{0:T(128)S(1)} %copy-done), kind=kLoop, calls=%fused_computation | loop fusion | flops 2097152 | bytes 2359328 | tf_op jit(solution)/shard_map/convert_element_type | solution.py:808
Async XLA Ops:
  0.0 33.5 %copy-start = (f32[8]{0:T(128)S(1)}, f32[8]{0:T(128)}, u32[]{:S(2)}) copy-start(f32[8]{0:T(128)} %gain_hbm.1) | copy-start | bytes 100

commit v4 on v3

--- a/solution.py
+++ b/solution.py
@@ -94,6 +94,8 @@
     mixed_hbm,
     pan_total,
     send_ref,
+    row_ref,
+    col_ref,
     mix_ref,
     gain_ref,
     synth_ref,
@@ -103,8 +105,8 @@
     ms_sum,
     table_ref,
     table,
-    rows_all,
-    cols_all,
+    nodes_ref,
+    nodes_all,
     ms_y_send,
     ms_y_recv,
     pan_y_send,
@@ -115,12 +117,9 @@
     pan_z_recv,
     near_ms_send,
     near_ms_recv,
-    near_pan_send,
-    near_pan_recv,
     ms_total,
     ms_hold,
-    pan_part_sum,
-    pan_hold,
+    ms_mine,
     window,
     rim_send,
     rim_recv,
@@ -133,10 +132,8 @@
     across,
     mixed,
     load_sem,
-    rows_ss,
-    rows_rs,
-    cols_ss,
-    cols_rs,
+    nodes_ss,
+    nodes_rs,
     ms_y_ss,
     ms_y_rs,
     pan_y_ss,
@@ -198,8 +195,8 @@
         pltpu.make_async_copy(src, dst, load_sem.at[k])
         for k, (src, dst) in enumerate(
             (
-                (row_hbm, rows_all.at[m]),
-                (col_hbm, cols_all.at[c, m]),
+                (row_hbm, row_ref),
+                (col_hbm, col_ref),
                 (send_hbm, send_ref),
                 (ms_hbm, ms_ref),
                 (pan_hbm, pan_ref),
@@ -213,30 +210,32 @@
         load.start()
     row_load, col_load, send_load, ms_load, pan_load, *late_loads = loads
 
+    nodes_ref[...] = jnp.zeros_like(nodes_ref)
+    row_load.wait()
+    col_load.wait()
+    nodes_ref[0:1, 0 : row_ref.shape[1]] = row_ref[...]
+    nodes_ref[1:2, 0 : col_ref.shape[1]] = col_ref[...]
+    nodes_all[c, m] = nodes_ref[...]
     pl.semaphore_wait(barrier, 2 * n - 1)
 
-    def rows_copy(slot, row):
-        return remote(row_hbm, rows_all.at[slot], rows_ss.at[row], rows_rs.at[slot], row, c)
-
-    def cols_copy(slot_row, slot_col, row, col):
+    def nodes_copy(slot_row, slot_col, row, col):
         return remote(
-            col_hbm,
-            cols_all.at[slot_col, slot_row],
-            cols_ss.at[col, row],
-            cols_rs.at[slot_col, slot_row],
+            nodes_ref,
+            nodes_all.at[slot_col, slot_row],
+            nodes_ss.at[col, row],
+            nodes_rs.at[slot_col, slot_row],
             row,
             col,
         )
 
     def send_nodes(k, carry):
         row = lax.rem(m + k, n)
-        cols_copy(m, c, row, other).start()
-        cols_copy(m, c, row, c).start()
-        rows_copy(m, row).start()
+        nodes_copy(m, c, row, c).start()
+        nodes_copy(m, c, row, other).start()
         return carry
 
     lax.fori_loop(1, n, send_nodes, 0)
-    cols_copy(m, c, m, other).start()
+    nodes_copy(m, c, m, other).start()
     send_load.wait()
 
     square = (own_blocks, own_blocks)
@@ -290,15 +289,12 @@
 
     def wait_nodes(k, carry):
         row = lax.rem(m + k, n)
-        cols_copy(row, c, row, c).wait()
-        cols_copy(row, other, row, other).wait()
-        rows_copy(row, row).wait()
+        nodes_copy(row, c, row, c).wait()
+        nodes_copy(row, other, row, other).wait()
         return carry
 
-    row_load.wait()
-    col_load.wait()
     lax.fori_loop(1, n, wait_nodes, 0)
-    cols_copy(m, other, m, other).wait()
+    nodes_copy(m, other, m, other).wait()
 
     def cell_of(sums, tile, row, col):
         cell = (tile * KR + row) * KC + col
@@ -308,8 +304,8 @@
         return jnp.concatenate([cell_of(sums, tile, row, col) for row in range(KR)], axis=0)
 
     def ms_part(tile):
-        row_nodes, nodes = rows_all[tile], cols_all[c, tile]
-        after = cols_all[1, tile][:, 0:1]
+        row_nodes, nodes = nodes_all[c, tile, 0:1], nodes_all[c, tile, 1:2]
+        after = nodes_all[1, tile, 1:2, 0:1]
         x_ms = col_coord(
             nodes, after, is_last, col_nodes, 4 * iota((1, coarse_cols), 1) + 1, 0.5
         )
@@ -331,8 +327,8 @@
         return jnp.dot(jnp.concatenate(by_band, axis=0), col, preferred_element_type=F32)
 
     def pan_part(tile):
-        row_nodes, nodes = rows_all[tile], cols_all[c, tile]
-        after = cols_all[1, tile][:, 0:1]
+        row_nodes, nodes = nodes_all[c, tile, 0:1], nodes_all[c, tile, 1:2]
+        after = nodes_all[1, tile, 1:2, 0:1]
         x_pan = col_coord(nodes, after, is_last, col_nodes, iota((1, TC), 1), 0.0)
         col = spread(x_pan, (first_col * size).astype(F32), KC * size)
         row = spread(row_coord(row_nodes, iota((1, TR), 1), 0.0), 0.0, KR * size)
@@ -407,12 +403,7 @@
 
     near_row = partner * 2 + y
 
-    def near(k, src, dst):
-        return remote(src, dst, near_ss.at[k], near_rs.at[k], near_row, c)
-
-    near_ms = near(0, near_ms_send, near_ms_recv)
-    near_pan = near(1, near_pan_send, near_pan_recv)
-    first_rows = slice(0, part_rows)
+    near_ms = remote(near_ms_send, near_ms_recv, near_ss, near_rs, near_row, c)
 
     def ms_twin_parts(k):
         return [ms_part(line_of(k + i) * 2 + 1 - y) for i in range(2)]
@@ -447,18 +438,18 @@
     def pan_onward(k):
         line = line_of(k)
         inner, row, slot = route(line)
-        pan_part_sum[...] = pan_part(line * 2 + y)
+        pan_total[...] = pan_part(line * 2 + y)
         for h in range(HALVES):
             rows = slice(h * part_rows, (h + 1) * part_rows)
             pan_y(k, h).wait_recv()
-            pan_part_sum[rows, :] += pan_y_recv[k, rows].astype(F32)
+            pan_total[rows, :] += pan_y_recv[k, rows].astype(F32)
 
             @pl.when(inner)
             def _():
                 pan_z(0, h, row, blocks + line).wait_recv()
-                pan_part_sum[rows, :] += pan_z_recv[blocks + line, rows].astype(F32)
-
-            pan_z_send[k, rows] = pan_part_sum[rows, :].astype(BF16)
+                pan_total[rows, :] += pan_z_recv[blocks + line, rows].astype(F32)
+
+            pan_z_send[k, rows] = pan_total[rows, :].astype(BF16)
             pan_z(k, h, row, slot).start()
 
     far = lines - 2
@@ -480,37 +471,17 @@
     near_ms_send[...] = parts[0].astype(BF16)
     ms_hold[...] = parts[1]
     near_ms.start()
-    pan_to_twin(0)
-    pan_y_send[far] = pan_twin_part(far).astype(BF16)
-    near_pan_send[...] = pan_y_send[far, first_rows]
-    near_pan.start()
-    each(1, far, pan_to_twin)
-    for h in range(1, HALVES):
-        pan_y(far, h).start()
-    pan_hold[...] = pan_twin_part(last)
+    ms_own_parts(far)
+    ms_z_send[far] = ms_total[0].astype(BF16)
+    ms_z(far, near_row, pair).start()
+    ms_mine[...] = ms_total[1]
+    each(0, far, pan_to_twin)
     near_ms.wait_recv()
     ms_y_send[last] = (ms_hold[...] + near_ms_recv[...].astype(F32)).astype(BF16)
     ms_y(last).start()
-    near_pan.wait_recv()
-    pan_hold[first_rows, :] += near_pan_recv[...].astype(F32)
-    pan_y_send[last] = pan_hold[...].astype(BF16)
-    for h in range(HALVES):
-        pan_y(last, h).start()
     each(0, far // 2, ms_far_onward)
-
-    early = route(line_of(far - 1))[0]
-    ms_own_parts(far)
-    ms_z_send[far] = ms_total[0].astype(BF16)
-    pan_hold[...] = pan_part(near_row)
-    pan_z_send[far, first_rows] = pan_hold[first_rows, :].astype(BF16)
-
-    def near_start():
-        ms_z(far, near_row, pair).start()
-        pan_z(far, 0, near_row, pair).start()
-
-    pl.when(early)(near_start)
+    each(far, lines, pan_to_twin)
     each(0, far, pan_onward)
-    pl.when(jnp.logical_not(early))(near_start)
 
     spot = (iota((coarse_cols, TC), 1).astype(F32) - 1.5) * 0.25 + 2.0
     tap = iota((coarse_cols, TC), 0) + 2
@@ -519,17 +490,17 @@
     up_cols[coarse_cols : coarse_cols + LANES, :] = cubic_weight(spot - tap.astype(F32)).astype(BF16)
 
     ms_y(last).wait_recv()
-    ms_total[1] += ms_y_recv[last].astype(F32)
+    ms_mine[...] += ms_y_recv[last].astype(F32)
 
     def ms_arrived(slot, carry):
         ms_z(0, m, slot).wait_recv()
-        ms_total[1] += ms_z_recv[slot].astype(F32)
+        ms_mine[...] += ms_z_recv[slot].astype(F32)
         return carry
 
     lax.fori_loop(0, blocks, ms_arrived, 0)
     for load in late_loads:
         load.wait()
-    values = [ms_total[1, b * coarse_rows : (b + 1) * coarse_rows, :] for b in range(bands)]
+    values = [ms_mine[b * coarse_rows : (b + 1) * coarse_rows, :] for b in range(bands)]
     synthetic = sum(synth_ref[b] * values[b] for b in range(bands))
     spot = iota((coarse_rows, LANES), 1) // 2
     edges = jnp.zeros((coarse_rows, LANES), F32)
@@ -576,12 +547,7 @@
         for copy in down_copies:
             copy.start()
 
-    for h in range(1, HALVES):
-        rows = slice(h * part_rows, (h + 1) * part_rows)
-        pan_y(far, h).wait_recv()
-        pan_hold[rows, :] += pan_y_recv[far, rows].astype(F32)
-        pan_z_send[far, rows] = pan_hold[rows, :].astype(BF16)
-        pan_z(far, h, near_row, pair).start()
+    pan_onward(far)
     pan_total[...] = pan_part(m)
     across_copy.wait()
 
@@ -669,13 +635,12 @@
 
         lax.fori_loop(0, blocks, pan_arrived, 0)
 
-    def y_sent(k, carry):
+    def ms_y_sent(k, carry):
         ms_y(k).wait_send()
-        pan_y(k, 0).wait_send()
         return carry
 
-    def y_rest_sent(k, carry):
-        for h in range(1, HALVES):
+    def pan_y_sent(k, carry):
+        for h in range(HALVES):
             pan_y(k, h).wait_send()
         return carry
 
@@ -686,10 +651,9 @@
         return carry
 
     near_ms.wait_send()
-    near_pan.wait_send()
-    lax.fori_loop(0, far, y_sent, 0)
-    lax.fori_loop(last, lines, y_sent, 0)
-    lax.fori_loop(0, lines, y_rest_sent, 0)
+    lax.fori_loop(0, far, ms_y_sent, 0)
+    ms_y(last).wait_send()
+    lax.fori_loop(0, lines, pan_y_sent, 0)
     lax.fori_loop(0, lines - 1, z_sent, 0)
     store.wait()
 
@@ -734,6 +698,8 @@
         out_specs=(hbm, vmem),
         scratch_shapes=[
             pltpu.VMEM(send_list.shape, I32),
+            pltpu.VMEM((1, row_grid.shape[0]), F32),
+            pltpu.VMEM(col_grid.shape, F32),
             pltpu.SMEM(band_mix.shape, F32),
             pltpu.SMEM(band_gain.shape, F32),
             pltpu.SMEM(synth_weight.shape, F32),
@@ -743,8 +709,8 @@
             pltpu.VMEM((own_blocks + 1, coarse_size, coarse_width), BF16),
             pltpu.VMEM((table_rows, LANES), I32),
             pltpu.SMEM((table_rows, LANES), I32),
-            pltpu.VMEM((n, 1, row_grid.shape[0]), F32),
-            pltpu.VMEM((2, n) + col_grid.shape, F32),
+            pltpu.VMEM((8, LANES), F32),
+            pltpu.VMEM((2, n, 8, LANES), F32),
             ms_slots(lines),
             ms_slots(lines),
             pan_slots(lines),
@@ -755,12 +721,9 @@
             pan_slots(slots),
             pltpu.VMEM((bands * coarse_rows, coarse_cols), BF16),
             pltpu.VMEM((bands * coarse_rows, coarse_cols), BF16),
-            pltpu.VMEM((TR // HALVES, TC), BF16),
-            pltpu.VMEM((TR // HALVES, TC), BF16),
             pltpu.VMEM((2, bands * coarse_rows, coarse_cols), F32),
             pltpu.VMEM((bands * coarse_rows, coarse_cols), F32),
-            pltpu.VMEM((TR, TC), F32),
-            pltpu.VMEM((TR, TC), F32),
+            pltpu.VMEM((bands * coarse_rows, coarse_cols), F32),
             pltpu.VMEM((bands, coarse_rows, coarse_cols), BF16),
             pltpu.VMEM((2, 2 * bands, LANES), BF16),
             pltpu.VMEM((2, 2 * bands, LANES), BF16),
@@ -773,8 +736,6 @@
             pltpu.VMEM((bands * coarse_rows, TC), BF16),
             pltpu.VMEM((bands, TR, TC), BF16),
             dma((10,)),
-            dma((n,)),
-            dma((n,)),
             dma((2, n)),
             dma((2, n)),
             dma((lines,)),
@@ -785,8 +746,8 @@
             dma((slots,)),
             dma((lines - 1, HALVES)),
             dma((slots, HALVES)),
-            dma((2,)),
-            dma((2,)),
+            dma,
+            dma,
             dma((5,)),
             dma((5,)),
         ],

time: 36.3 us -> 35 us (0.964)
  Pallas kernels: 33.5 us -> 32.2 us
    pallas_call x1, Pallas kernels: 33.5 us -> 32.2 us  [local(): pl.pallas_call(functools.partial(mapping, capacity, col_grid.shape[1]), o...]
where the time goes in v4:
time: 35 us; the launch traced here: 34.9 us
  Pallas kernels  32.2 us (92%)
  other arithmetic  2.61 us (7%)
    pallas_call x1, Pallas kernels, local(): pl.pallas_call(functools.partial(mapping, capacity, col_grid.shape[1]), o...  32.2 us
    convert_element_type x1, other arithmetic, local(): return (mixed.astype(F32) + detail).astype(BF16)  2.61 us

profile of v4, /device:TPU:0, one launch (start us, length us, event | category | flops | bytes accessed | tf_op | source)
XLA Modules:
  0.0 34.9 jit_solution(3303044756682609431)
XLA Ops:
  0.0 0.0 copy-start
  0.0 32.2 %mapping.1 = (bf16[8,128,512]{2,1,0:T(8,128)(2,1)}, f32[128,512]{1,0:T(8,128)}) custom-call(s32[3,64]{1,0:T(4,128)} %send_hbm.1, f32[1,3]{1,0:T(1,128)} %bitcast.1, f32[1,8]{1,0:T(1,128)} %col_hbm.1, bf16[64,128,128]{2,1,0:T(8,128)(2,1)} %pan_hbm.1, bf16[64,32,256]{2,1,0:T(8,128)(2,1)} %ms_hbm.1, f32[8,8]{1,0:T(8,128)} %mix_hbm.1, f32[8]{0:T(128)} %gain_hbm.1, ...), custom_call_target="tpu_custom_call" | custom-call | tf_op jit(solution)/shard_map/mapping/pallas_call | solution.py:691
  32.2 0.0 copy-done
  32.2 2.6 %add_convert_fusion = bf16[8,128,512]{2,1,0:T(8,128)(2,1)} fusion(bf16[8,128,512]{2,1,0:T(8,128)(2,1)} %get-tuple-element.7, f32[128,512]{1,0:T(8,128)} %get-tuple-element.8, f32[8]{0:T(128)S(1)} %copy-done), kind=kLoop, calls=%fused_computation | loop fusion | flops 2097152 | bytes 2359328 | tf_op jit(solution)/shard_map/convert_element_type | solution.py:769
Async XLA Ops:
  0.0 32.2 %copy-start = (f32[8]{0:T(128)S(1)}, f32[8]{0:T(128)}, u32[]{:S(2)}) copy-start(f32[8]{0:T(128)} %gain_hbm.1) | copy-start | bytes 100

commit v5 on v4

--- a/solution.py
+++ b/solution.py
@@ -92,7 +92,7 @@
     gain_hbm,
     synth_hbm,
     mixed_hbm,
-    pan_total,
+    pan_hbm_out,
     send_ref,
     row_ref,
     col_ref,
@@ -117,9 +117,11 @@
     pan_z_recv,
     near_ms_send,
     near_ms_recv,
+    pan_total,
     ms_total,
     ms_hold,
     ms_mine,
+    pan_mine,
     window,
     rim_send,
     rim_recv,
@@ -189,8 +191,10 @@
         pl.semaphore_signal(barrier, inc=1, device_id=at(row, other), device_id_type=MESH)
         return carry
 
-    pl.semaphore_signal(barrier, inc=1, device_id=at(m, other), device_id_type=MESH)
-    lax.fori_loop(1, n, greet, 0)
+    def greet_all():
+        pl.semaphore_signal(barrier, inc=1, device_id=at(m, other), device_id_type=MESH)
+        lax.fori_loop(1, n, greet, 0)
+
     loads = [
         pltpu.make_async_copy(src, dst, load_sem.at[k])
         for k, (src, dst) in enumerate(
@@ -206,9 +210,12 @@
             )
         )
     ]
-    for load in loads:
+    row_load, col_load, send_load, ms_load, pan_load, *late_loads = loads
+    row_load.start()
+    col_load.start()
+    greet_all()
+    for load in loads[2:]:
         load.start()
-    row_load, col_load, send_load, ms_load, pan_load, *late_loads = loads
 
     nodes_ref[...] = jnp.zeros_like(nodes_ref)
     row_load.wait()
@@ -435,10 +442,12 @@
         ms_z_send[k] = ms_total[i].astype(BF16)
         ms_z(k, row, slot).start()
 
-    def pan_onward(k):
+    def pan_own_part(k):
+        pan_total[...] = pan_part(line_of(k) * 2 + y)
+
+    def pan_forward(k):
         line = line_of(k)
         inner, row, slot = route(line)
-        pan_total[...] = pan_part(line * 2 + y)
         for h in range(HALVES):
             rows = slice(h * part_rows, (h + 1) * part_rows)
             pan_y(k, h).wait_recv()
@@ -451,6 +460,10 @@
 
             pan_z_send[k, rows] = pan_total[rows, :].astype(BF16)
             pan_z(k, h, row, slot).start()
+
+    def pan_onward(k):
+        pan_own_part(k)
+        pan_forward(k)
 
     far = lines - 2
     last = lines - 1
@@ -479,47 +492,17 @@
     near_ms.wait_recv()
     ms_y_send[last] = (ms_hold[...] + near_ms_recv[...].astype(F32)).astype(BF16)
     ms_y(last).start()
-    each(0, far // 2, ms_far_onward)
-    each(far, lines, pan_to_twin)
-    each(0, far, pan_onward)
-
     spot = (iota((coarse_cols, TC), 1).astype(F32) - 1.5) * 0.25 + 2.0
     tap = iota((coarse_cols, TC), 0) + 2
     up_cols[0:coarse_cols, :] = cubic_weight(spot - tap.astype(F32)).astype(BF16)
     tap = iota((LANES, TC), 0) % 2 + jnp.where(c == 0, coarse_cols + 2, 0)
     up_cols[coarse_cols : coarse_cols + LANES, :] = cubic_weight(spot - tap.astype(F32)).astype(BF16)
 
-    ms_y(last).wait_recv()
-    ms_mine[...] += ms_y_recv[last].astype(F32)
-
-    def ms_arrived(slot, carry):
-        ms_z(0, m, slot).wait_recv()
-        ms_mine[...] += ms_z_recv[slot].astype(F32)
-        return carry
-
-    lax.fori_loop(0, blocks, ms_arrived, 0)
-    for load in late_loads:
-        load.wait()
-    values = [ms_mine[b * coarse_rows : (b + 1) * coarse_rows, :] for b in range(bands)]
-    synthetic = sum(synth_ref[b] * values[b] for b in range(bands))
-    spot = iota((coarse_rows, LANES), 1) // 2
-    edges = jnp.zeros((coarse_rows, LANES), F32)
-    tops, bottoms = [], []
-    for b in range(bands):
-        result = values[b] - gain_ref[b] * synthetic
-        for k in range(bands):
-            result = result + mix_ref[b, k] * values[k]
-        window[b] = result.astype(BF16)
-        moved = pltpu.roll(result, jnp.where(c == 0, 2 * b + 2, 2 * b), 1)
-        edges = jnp.where(spot == b, moved, edges)
-        tops.append(result[0:2, :])
-        bottoms.append(result[coarse_rows - 2 : coarse_rows, :])
-    edge_own[...] = edges.astype(BF16)
-    rim_send[0] = jnp.concatenate(tops, axis=0).astype(BF16)
-    rim_send[1] = jnp.concatenate(bottoms, axis=0).astype(BF16)
-    edge_send[0] = jnp.concatenate([edges[0:2, :]] * bands, axis=0).astype(BF16)
-    bottom = edges[coarse_rows - 2 : coarse_rows, :]
-    edge_send[1] = jnp.concatenate([bottom] * bands, axis=0).astype(BF16)
+    each(0, far // 2, ms_far_onward)
+    each(far, lines, pan_to_twin)
+    each(0, far - 1, pan_onward)
+    pan_mine[...] = pan_part(m)
+    pan_own_part(far - 1)
 
     has_above, has_below = m > 0, m < n - 1
 
@@ -535,20 +518,57 @@
         halo_copy(3, rim_send.at[1], rim_recv.at[0], m + 1, c),
         halo_copy(4, edge_send.at[1], edge_recv.at[0], m + 1, other),
     ]
-    across_copy.start()
-
-    @pl.when(has_above)
-    def _():
-        for copy in up_copies:
-            copy.start()
-
-    @pl.when(has_below)
-    def _():
-        for copy in down_copies:
-            copy.start()
-
-    pan_onward(far)
-    pan_total[...] = pan_part(m)
+    def ms_finish():
+        ms_y(last).wait_recv()
+        ms_mine[...] += ms_y_recv[last].astype(F32)
+
+        def ms_arrived(slot, carry):
+            ms_z(0, m, slot).wait_recv()
+            ms_mine[...] += ms_z_recv[slot].astype(F32)
+            return carry
+
+        lax.fori_loop(0, blocks, ms_arrived, 0)
+        values = [ms_mine[b * coarse_rows : (b + 1) * coarse_rows, :] for b in range(bands)]
+        synthetic = sum(synth_ref[b] * values[b] for b in range(bands))
+        spot = iota((coarse_rows, LANES), 1) // 2
+        edges = jnp.zeros((coarse_rows, LANES), F32)
+        tops, bottoms = [], []
+        for b in range(bands):
+            result = values[b] - gain_ref[b] * synthetic
+            for k in range(bands):
+                result = result + mix_ref[b, k] * values[k]
+            window[b] = result.astype(BF16)
+            moved = pltpu.roll(result, jnp.where(c == 0, 2 * b + 2, 2 * b), 1)
+            edges = jnp.where(spot == b, moved, edges)
+            tops.append(result[0:2, :])
+            bottoms.append(result[coarse_rows - 2 : coarse_rows, :])
+        edge_own[...] = edges.astype(BF16)
+        rim_send[0] = jnp.concatenate(tops, axis=0).astype(BF16)
+        rim_send[1] = jnp.concatenate(bottoms, axis=0).astype(BF16)
+        edge_send[0] = jnp.concatenate([edges[0:2, :]] * bands, axis=0).astype(BF16)
+        bottom = edges[coarse_rows - 2 : coarse_rows, :]
+        edge_send[1] = jnp.concatenate([bottom] * bands, axis=0).astype(BF16)
+
+        across_copy.start()
+
+        @pl.when(has_above)
+        def _():
+            for copy in up_copies:
+                copy.start()
+
+        @pl.when(has_below)
+        def _():
+            for copy in down_copies:
+                copy.start()
+
+    early = route(line_of(far - 1))[0]
+    for load in late_loads:
+        load.wait()
+    pl.when(early)(ms_finish)
+    pan_forward(far - 1)
+    pan_own_part(far)
+    pl.when(jnp.logical_not(early))(ms_finish)
+    pan_forward(far)
     across_copy.wait()
 
     edges = edge_all[...]
@@ -623,17 +643,23 @@
 
     store = pltpu.make_async_copy(mixed, mixed_hbm, load_sem.at[9])
     store.start()
+    pan_stores = []
     for h in range(HALVES):
         rows = slice(h * part_rows, (h + 1) * part_rows)
         pan_y(last, h).wait_recv()
-        pan_total[rows, :] += pan_y_recv[last, rows].astype(F32)
+        pan_mine[rows, :] += pan_y_recv[last, rows].astype(F32)
 
         def pan_arrived(slot, carry):
             pan_z(0, h, m, slot).wait_recv()
-            pan_total[rows, :] += pan_z_recv[slot, rows].astype(F32)
+            pan_mine[rows, :] += pan_z_recv[slot, rows].astype(F32)
             return carry
 
         lax.fori_loop(0, blocks, pan_arrived, 0)
+        part = pl.ds(h * part_rows, part_rows)
+        pan_stores.append(
+            pltpu.make_async_copy(pan_mine.at[part], pan_hbm_out.at[part], load_sem.at[10 + h])
+        )
+        pan_stores[-1].start()
 
     def ms_y_sent(k, carry):
         ms_y(k).wait_send()
@@ -656,6 +682,8 @@
     lax.fori_loop(0, lines, pan_y_sent, 0)
     lax.fori_loop(0, lines - 1, z_sent, 0)
     store.wait()
+    for pan_store in pan_stores:
+        pan_store.wait()
 
 
 def local(
@@ -677,7 +705,6 @@
     bands = band_gain.shape[0]
     coarse_rows, coarse_cols = TR // 4, TC // 4
     table_rows = pl.cdiv(2 + pl.cdiv(n * KR * KC, LANES), 8) * 8
-    vmem = pl.BlockSpec(memory_space=pltpu.VMEM)
     hbm = pl.BlockSpec(memory_space=pl.ANY)
     dma = pltpu.SemaphoreType.DMA
     slots = lines // 2 + lines
@@ -695,7 +722,7 @@
             jax.ShapeDtypeStruct((TR, TC), F32),
         ),
         in_specs=[hbm] * 8,
-        out_specs=(hbm, vmem),
+        out_specs=(hbm, hbm),
         scratch_shapes=[
             pltpu.VMEM(send_list.shape, I32),
             pltpu.VMEM((1, row_grid.shape[0]), F32),
@@ -721,9 +748,11 @@
             pan_slots(slots),
             pltpu.VMEM((bands * coarse_rows, coarse_cols), BF16),
             pltpu.VMEM((bands * coarse_rows, coarse_cols), BF16),
+            pltpu.VMEM((TR, TC), F32),
             pltpu.VMEM((2, bands * coarse_rows, coarse_cols), F32),
             pltpu.VMEM((bands * coarse_rows, coarse_cols), F32),
             pltpu.VMEM((bands * coarse_rows, coarse_cols), F32),
+            pltpu.VMEM((TR, TC), F32),
             pltpu.VMEM((bands, coarse_rows, coarse_cols), BF16),
             pltpu.VMEM((2, 2 * bands, LANES), BF16),
             pltpu.VMEM((2, 2 * bands, LANES), BF16),
@@ -735,7 +764,7 @@
             pltpu.VMEM((TR, coarse_rows + 4 * bands), BF16),
             pltpu.VMEM((bands * coarse_rows, TC), BF16),
             pltpu.VMEM((bands, TR, TC), BF16),
-            dma((10,)),
+            dma((10 + HALVES,)),
             dma((2, n)),
             dma((2, n)),
             dma((lines,)),

time: 35 us -> 34.6 us (0.989)
    pallas_call x1, Pallas kernels: 32.2 us -> 31.9 us  [local(): pl.pallas_call(functools.partial(mapping, capacity, col_grid.shape[1]), o...]
where the time goes in v5:
time: 34.6 us; the launch traced here: 34.5 us
  Pallas kernels  31.9 us (92%)
  other arithmetic  2.61 us (8%)
    pallas_call x1, Pallas kernels, local(): pl.pallas_call(functools.partial(mapping, capacity, col_grid.shape[1]), o...  31.9 us
    convert_element_type x1, other arithmetic, local(): return (mixed.astype(F32) + detail).astype(BF16)  2.61 us

profile of v5, /device:TPU:0, one launch (start us, length us, event | category | flops | bytes accessed | tf_op | source)
XLA Modules:
  0.0 34.5 jit_solution(4633108300510876897)
XLA Ops:
  0.0 0.0 copy-start
  0.0 31.9 %mapping.1 = (bf16[8,128,512]{2,1,0:T(8,128)(2,1)}, f32[128,512]{1,0:T(8,128)}) custom-call(s32[3,64]{1,0:T(4,128)} %send_hbm.1, f32[1,3]{1,0:T(1,128)} %bitcast.1, f32[1,8]{1,0:T(1,128)} %col_hbm.1, bf16[64,128,128]{2,1,0:T(8,128)(2,1)} %pan_hbm.1, bf16[64,32,256]{2,1,0:T(8,128)(2,1)} %ms_hbm.1, f32[8,8]{1,0:T(8,128)} %mix_hbm.1, f32[8]{0:T(128)} %gain_hbm.1, ...), custom_call_target="tpu_custom_call" | custom-call | tf_op jit(solution)/shard_map/mapping/pallas_call | solution.py:718
  31.9 0.0 copy-done
  31.9 2.6 %add_convert_fusion = bf16[8,128,512]{2,1,0:T(8,128)(2,1)} fusion(bf16[8,128,512]{2,1,0:T(8,128)(2,1)} %get-tuple-element.7, f32[128,512]{1,0:T(8,128)} %get-tuple-element.8, f32[8]{0:T(128)S(1)} %copy-done), kind=kLoop, calls=%fused_computation | loop fusion | flops 2097152 | bytes 2359328 | tf_op jit(solution)/shard_map/convert_element_type | solution.py:798
Async XLA Ops:
  0.0 31.9 %copy-start = (f32[8]{0:T(128)S(1)}, f32[8]{0:T(128)}, u32[]{:S(2)}) copy-start(f32[8]{0:T(128)} %gain_hbm.1) | copy-start | bytes 100

commit v6 on v5

--- a/solution.py
+++ b/solution.py
@@ -12,7 +12,8 @@
 TC = 512
 KR = 2
 KC = 5
-LANES = 128
+LANE_BITS = 7
+LANES = 1 << LANE_BITS
 PACK = 16
 HALVES = 2
 MESH = pl.DeviceIdType.MESH
@@ -276,6 +277,14 @@
     )
     spot = (iota(up_rows.shape, 0).astype(F32) - 1.5) * 0.25 + 2.0
     up_rows[...] = cubic_weight(spot - tap.astype(F32)).astype(BF16)
+    spot = (iota((1, TC), 1).astype(F32) - 1.5) * 0.25 + 2.0
+    up_cols[0:coarse_cols, :] = spread(spot, 2.0, coarse_cols)
+    start = jnp.where(c == 0, coarse_cols + 2, 0).astype(F32)
+    shape = (PACK, TC)
+    beside = [jnp.broadcast_to(cubic_weight(spot - (start + e)), shape) for e in (0.0, 1.0)]
+    beside = jnp.where(iota(shape, 0) % 2 == 0, beside[0], beside[1]).astype(BF16)
+    for g in range(LANES // PACK):
+        up_cols[coarse_cols + g * PACK : coarse_cols + (g + 1) * PACK, :] = beside
     pan_sum[0] = jnp.zeros((size, size), BF16)
     ms_sum[0] = jnp.zeros((coarse_size, coarse_width), BF16)
     table_copy.wait()
@@ -304,8 +313,10 @@
     nodes_copy(m, other, m, other).wait()
 
     def cell_of(sums, tile, row, col):
-        cell = (tile * KR + row) * KC + col
-        return sums[table[2 + cell // LANES, cell % LANES]]
+        cell = tile * (KR * KC) + (row * KC + col)
+        if cells <= LANES:
+            return sums[table[2, cell]]
+        return sums[table[2 + (cell >> LANE_BITS), cell & (LANES - 1)]]
 
     def stacked(sums, tile, col):
         return jnp.concatenate([cell_of(sums, tile, row, col) for row in range(KR)], axis=0)
@@ -415,13 +426,13 @@
     def ms_twin_parts(k):
         return [ms_part(line_of(k + i) * 2 + 1 - y) for i in range(2)]
 
-    def pan_twin_part(k):
-        return pan_part(line_of(k) * 2 + 1 - y)
-
-    def pan_to_twin(k):
-        pan_y_send[k] = pan_twin_part(k).astype(BF16)
-        for h in range(HALVES):
-            pan_y(k, h).start()
+    def pan_pair_to_twin(p):
+        parts = [pan_part(line_of(2 * p + i) * 2 + 1 - y) for i in range(2)]
+        for i, part in enumerate(parts):
+            pan_y_send[2 * p + i] = part.astype(BF16)
+        for i in range(2):
+            for h in range(HALVES):
+                pan_y(2 * p + i, h).start()
 
     def ms_own_parts(k):
         parts = [ms_part(line_of(k + i) * 2 + y) for i in range(2)]
@@ -432,14 +443,18 @@
         line = line_of(k)
         inner, row, slot = route(line)
         ms_y(k).wait_recv()
-        ms_total[i] += ms_y_recv[k].astype(F32)
 
         @pl.when(inner)
         def _():
             ms_z(0, row, blocks + line).wait_recv()
-            ms_total[i] += ms_z_recv[blocks + line].astype(F32)
-
-        ms_z_send[k] = ms_total[i].astype(BF16)
+            relayed = ms_z_recv[blocks + line].astype(F32)
+            total = ms_total[i] + ms_y_recv[k].astype(F32)
+            ms_z_send[k] = (total + relayed).astype(BF16)
+
+        @pl.when(jnp.logical_not(inner))
+        def _():
+            ms_z_send[k] = (ms_total[i] + ms_y_recv[k].astype(F32)).astype(BF16)
+
         ms_z(k, row, slot).start()
 
     def pan_own_part(k):
@@ -451,14 +466,19 @@
         for h in range(HALVES):
             rows = slice(h * part_rows, (h + 1) * part_rows)
             pan_y(k, h).wait_recv()
-            pan_total[rows, :] += pan_y_recv[k, rows].astype(F32)
 
             @pl.when(inner)
             def _():
                 pan_z(0, h, row, blocks + line).wait_recv()
-                pan_total[rows, :] += pan_z_recv[blocks + line, rows].astype(F32)
-
-            pan_z_send[k, rows] = pan_total[rows, :].astype(BF16)
+                relayed = pan_z_recv[blocks + line, rows].astype(F32)
+                total = pan_total[rows, :] + pan_y_recv[k, rows].astype(F32)
+                pan_z_send[k, rows] = (total + relayed).astype(BF16)
+
+            @pl.when(jnp.logical_not(inner))
+            def _():
+                total = pan_total[rows, :] + pan_y_recv[k, rows].astype(F32)
+                pan_z_send[k, rows] = total.astype(BF16)
+
             pan_z(k, h, row, slot).start()
 
     def pan_onward(k):
@@ -484,22 +504,16 @@
     near_ms_send[...] = parts[0].astype(BF16)
     ms_hold[...] = parts[1]
     near_ms.start()
+    each(0, far // 2, pan_pair_to_twin)
     ms_own_parts(far)
     ms_z_send[far] = ms_total[0].astype(BF16)
     ms_z(far, near_row, pair).start()
     ms_mine[...] = ms_total[1]
-    each(0, far, pan_to_twin)
+    each(0, far // 2, ms_far_onward)
     near_ms.wait_recv()
     ms_y_send[last] = (ms_hold[...] + near_ms_recv[...].astype(F32)).astype(BF16)
     ms_y(last).start()
-    spot = (iota((coarse_cols, TC), 1).astype(F32) - 1.5) * 0.25 + 2.0
-    tap = iota((coarse_cols, TC), 0) + 2
-    up_cols[0:coarse_cols, :] = cubic_weight(spot - tap.astype(F32)).astype(BF16)
-    tap = iota((LANES, TC), 0) % 2 + jnp.where(c == 0, coarse_cols + 2, 0)
-    up_cols[coarse_cols : coarse_cols + LANES, :] = cubic_weight(spot - tap.astype(F32)).astype(BF16)
-
-    each(0, far // 2, ms_far_onward)
-    each(far, lines, pan_to_twin)
+    pan_pair_to_twin(far // 2)
     each(0, far - 1, pan_onward)
     pan_mine[...] = pan_part(m)
     pan_own_part(far - 1)

time: 34.6 us -> 34.1 us (0.986)
  Pallas kernels: 31.9 us -> 31.3 us
    pallas_call x1, Pallas kernels: 31.9 us -> 31.3 us  [local(): pl.pallas_call(functools.partial(mapping, capacity, col_grid.shape[1]), o...]
where the time goes in v6:
time: 34.1 us; the launch traced here: 34 us
  Pallas kernels  31.3 us (92%)
  other arithmetic  2.61 us (8%)
    pallas_call x1, Pallas kernels, local(): pl.pallas_call(functools.partial(mapping, capacity, col_grid.shape[1]), o...  31.3 us
    convert_element_type x1, other arithmetic, local(): return (mixed.astype(F32) + detail).astype(BF16)  2.61 us

profile of v6, /device:TPU:0, one launch (start us, length us, event | category | flops | bytes accessed | tf_op | source)
XLA Modules:
  0.0 34.0 jit_solution(3688453075835273796)
XLA Ops:
  0.0 0.0 copy-start
  0.0 31.3 %mapping.1 = (bf16[8,128,512]{2,1,0:T(8,128)(2,1)}, f32[128,512]{1,0:T(8,128)}) custom-call(s32[3,64]{1,0:T(4,128)} %send_hbm.1, f32[1,3]{1,0:T(1,128)} %bitcast.1, f32[1,8]{1,0:T(1,128)} %col_hbm.1, bf16[64,128,128]{2,1,0:T(8,128)(2,1)} %pan_hbm.1, bf16[64,32,256]{2,1,0:T(8,128)(2,1)} %ms_hbm.1, f32[8,8]{1,0:T(8,128)} %mix_hbm.1, f32[8]{0:T(128)} %gain_hbm.1, ...), custom_call_target="tpu_custom_call" | custom-call | tf_op jit(solution)/shard_map/mapping/pallas_call | solution.py:732
  31.3 0.0 copy-done
  31.4 2.6 %add_convert_fusion = bf16[8,128,512]{2,1,0:T(8,128)(2,1)} fusion(bf16[8,128,512]{2,1,0:T(8,128)(2,1)} %get-tuple-element.7, f32[128,512]{1,0:T(8,128)} %get-tuple-element.8, f32[8]{0:T(128)S(1)} %copy-done), kind=kLoop, calls=%fused_computation | loop fusion | flops 2097152 | bytes 2359328 | tf_op jit(solution)/shard_map/convert_element_type | solution.py:812
Async XLA Ops:
  0.0 31.4 %copy-start = (f32[8]{0:T(128)S(1)}, f32[8]{0:T(128)}, u32[]{:S(2)}) copy-start(f32[8]{0:T(128)} %gain_hbm.1) | copy-start | bytes 100

commit v7 on v6

--- a/solution.py
+++ b/solution.py
@@ -426,13 +426,21 @@
     def ms_twin_parts(k):
         return [ms_part(line_of(k + i) * 2 + 1 - y) for i in range(2)]
 
+    swap = route(line_of(lines - 3))[0]
+
+    def pan_turn(k):
+        first = jnp.where(swap, lines - 2, lines - 3)
+        second = jnp.where(swap, lines - 3, lines - 2)
+        return jnp.where(k == lines - 3, first, jnp.where(k == lines - 2, second, k))
+
     def pan_pair_to_twin(p):
-        parts = [pan_part(line_of(2 * p + i) * 2 + 1 - y) for i in range(2)]
-        for i, part in enumerate(parts):
-            pan_y_send[2 * p + i] = part.astype(BF16)
-        for i in range(2):
+        keys = [pan_turn(2 * p + i) for i in range(2)]
+        parts = [pan_part(line_of(k) * 2 + 1 - y) for k in keys]
+        for k, part in zip(keys, parts):
+            pan_y_send[k] = part.astype(BF16)
+        for k in keys:
             for h in range(HALVES):
-                pan_y(2 * p + i, h).start()
+                pan_y(k, h).start()
 
     def ms_own_parts(k):
         parts = [ms_part(line_of(k + i) * 2 + y) for i in range(2)]
@@ -516,7 +524,7 @@
     pan_pair_to_twin(far // 2)
     each(0, far - 1, pan_onward)
     pan_mine[...] = pan_part(m)
-    pan_own_part(far - 1)
+    pan_own_part(pan_turn(far - 1))
 
     has_above, has_below = m > 0, m < n - 1
 
@@ -575,14 +583,12 @@
             for copy in down_copies:
                 copy.start()
 
-    early = route(line_of(far - 1))[0]
     for load in late_loads:
         load.wait()
-    pl.when(early)(ms_finish)
-    pan_forward(far - 1)
-    pan_own_part(far)
-    pl.when(jnp.logical_not(early))(ms_finish)
-    pan_forward(far)
+    pan_forward(pan_turn(far - 1))
+    pan_own_part(pan_turn(far))
+    ms_finish()
+    pan_forward(pan_turn(far))
     across_copy.wait()
 
     edges = edge_all[...]

time: 34.1 us -> 33 us (0.968)
  Pallas kernels: 31.3 us -> 30 us
    pallas_call x1, Pallas kernels: 31.3 us -> 30 us  [local(): pl.pallas_call(functools.partial(mapping, capacity, col_grid.shape[1]), o...]
where the time goes in v7:
time: 33 us; the launch traced here: 32.7 us
  Pallas kernels  30 us (91%)
  other arithmetic  2.61 us (8%)
    pallas_call x1, Pallas kernels, local(): pl.pallas_call(functools.partial(mapping, capacity, col_grid.shape[1]), o...  30 us
    convert_element_type x1, other arithmetic, local(): return (mixed.astype(F32) + detail).astype(BF16)  2.61 us

profile of v7, /device:TPU:0, one launch (start us, length us, event | category | flops | bytes accessed | tf_op | source)
XLA Modules:
  0.0 32.7 jit_solution(6874313233788067115)
XLA Ops:
  0.0 0.0 copy-start
  0.0 30.0 %mapping.1 = (bf16[8,128,512]{2,1,0:T(8,128)(2,1)}, f32[128,512]{1,0:T(8,128)}) custom-call(s32[3,64]{1,0:T(4,128)} %send_hbm.1, f32[1,3]{1,0:T(1,128)} %bitcast.1, f32[1,8]{1,0:T(1,128)} %col_hbm.1, bf16[64,128,128]{2,1,0:T(8,128)(2,1)} %pan_hbm.1, bf16[64,32,256]{2,1,0:T(8,128)(2,1)} %ms_hbm.1, f32[8,8]{1,0:T(8,128)} %mix_hbm.1, f32[8]{0:T(128)} %gain_hbm.1, ...), custom_call_target="tpu_custom_call" | custom-call | tf_op jit(solution)/shard_map/mapping/pallas_call | solution.py:738
  30.0 0.0 copy-done
  30.0 2.6 %add_convert_fusion = bf16[8,128,512]{2,1,0:T(8,128)(2,1)} fusion(bf16[8,128,512]{2,1,0:T(8,128)(2,1)} %get-tuple-element.7, f32[128,512]{1,0:T(8,128)} %get-tuple-element.8, f32[8]{0:T(128)S(1)} %copy-done), kind=kLoop, calls=%fused_computation | loop fusion | flops 2097152 | bytes 2359328 | tf_op jit(solution)/shard_map/convert_element_type | solution.py:818
Async XLA Ops:
  0.0 30.0 %copy-start = (f32[8]{0:T(128)S(1)}, f32[8]{0:T(128)}, u32[]{:S(2)}) copy-start(f32[8]{0:T(128)} %gain_hbm.1) | copy-start | bytes 100

commit v8 on v7

--- a/solution.py
+++ b/solution.py
@@ -613,6 +613,17 @@
             preferred_element_type=F32,
         ).astype(BF16)
 
+    spans = ((PACK, TR - 2 * PACK), (0, PACK), (TR - PACK, PACK))
+    stores = []
+    for k, (begin, count) in enumerate(spans):
+        span = pl.ds(begin, count)
+        stores.append(
+            pltpu.make_async_copy(
+                mixed.at[:, span], mixed_hbm.at[:, span], load_sem.at[9 + k]
+            )
+        )
+    stores[0].start()
+
     @pl.when(has_above)
     def _():
         for copy in up_copies:
@@ -661,8 +672,8 @@
         mixed[b, 0:PACK, :] = ends[0:PACK, :]
         mixed[b, TR - PACK : TR, :] = ends[PACK : 2 * PACK, :]
 
-    store = pltpu.make_async_copy(mixed, mixed_hbm, load_sem.at[9])
-    store.start()
+    for k in (1, 2):
+        stores[k].start()
     pan_stores = []
     for h in range(HALVES):
         rows = slice(h * part_rows, (h + 1) * part_rows)
@@ -677,7 +688,7 @@
         lax.fori_loop(0, blocks, pan_arrived, 0)
         part = pl.ds(h * part_rows, part_rows)
         pan_stores.append(
-            pltpu.make_async_copy(pan_mine.at[part], pan_hbm_out.at[part], load_sem.at[10 + h])
+            pltpu.make_async_copy(pan_mine.at[part], pan_hbm_out.at[part], load_sem.at[12 + h])
         )
         pan_stores[-1].start()
 
@@ -701,7 +712,8 @@
     ms_y(last).wait_send()
     lax.fori_loop(0, lines, pan_y_sent, 0)
     lax.fori_loop(0, lines - 1, z_sent, 0)
-    store.wait()
+    for store in stores:
+        store.wait()
     for pan_store in pan_stores:
         pan_store.wait()
 
@@ -756,8 +768,8 @@
             pltpu.VMEM((own_blocks + 1, coarse_size, coarse_width), BF16),
             pltpu.VMEM((table_rows, LANES), I32),
             pltpu.SMEM((table_rows, LANES), I32),
-            pltpu.VMEM((8, LANES), F32),
-            pltpu.VMEM((2, n, 8, LANES), F32),
+            pltpu.VMEM((2, LANES), F32),
+            pltpu.VMEM((2, n, 2, LANES), F32),
             ms_slots(lines),
             ms_slots(lines),
             pan_slots(lines),
@@ -784,7 +796,7 @@
             pltpu.VMEM((TR, coarse_rows + 4 * bands), BF16),
             pltpu.VMEM((bands * coarse_rows, TC), BF16),
             pltpu.VMEM((bands, TR, TC), BF16),
-            dma((10 + HALVES,)),
+            dma((12 + HALVES,)),
             dma((2, n)),
             dma((2, n)),
             dma((lines,)),

time: 33 us -> 32.7 us (level)
    pallas_call x1, Pallas kernels: 30 us -> 29.7 us  [local(): pl.pallas_call(functools.partial(mapping, capacity, col_grid.shape[1]), o...]
where the time goes in v8:
time: 32.7 us; the launch traced here: 32.3 us
  Pallas kernels  29.7 us (91%)
  other arithmetic  2.61 us (8%)
    pallas_call x1, Pallas kernels, local(): pl.pallas_call(functools.partial(mapping, capacity, col_grid.shape[1]), o...  29.7 us
    convert_element_type x1, other arithmetic, local(): return (mixed.astype(F32) + detail).astype(BF16)  2.61 us

profile of v8, /device:TPU:0, one launch (start us, length us, event | category | flops | bytes accessed | tf_op | source)
XLA Modules:
  0.0 32.3 jit_solution(689754393971074383)
XLA Ops:
  0.0 0.0 copy-start
  0.0 29.7 %mapping.1 = (bf16[8,128,512]{2,1,0:T(8,128)(2,1)}, f32[128,512]{1,0:T(8,128)}) custom-call(s32[3,64]{1,0:T(4,128)} %send_hbm.1, f32[1,3]{1,0:T(1,128)} %bitcast.1, f32[1,8]{1,0:T(1,128)} %col_hbm.1, bf16[64,128,128]{2,1,0:T(8,128)(2,1)} %pan_hbm.1, bf16[64,32,256]{2,1,0:T(8,128)(2,1)} %ms_hbm.1, f32[8,8]{1,0:T(8,128)} %mix_hbm.1, f32[8]{0:T(128)} %gain_hbm.1, ...), custom_call_target="tpu_custom_call" | custom-call | tf_op jit(solution)/shard_map/mapping/pallas_call | solution.py:750
  29.7 0.0 copy-done
  29.7 2.6 %add_convert_fusion = bf16[8,128,512]{2,1,0:T(8,128)(2,1)} fusion(bf16[8,128,512]{2,1,0:T(8,128)(2,1)} %get-tuple-element.7, f32[128,512]{1,0:T(8,128)} %get-tuple-element.8, f32[8]{0:T(128)S(1)} %copy-done), kind=kLoop, calls=%fused_computation | loop fusion | flops 2097152 | bytes 2359328 | tf_op jit(solution)/shard_map/convert_element_type | solution.py:830
Async XLA Ops:
  0.0 29.7 %copy-start = (f32[8]{0:T(128)S(1)}, f32[8]{0:T(128)}, u32[]{:S(2)}) copy-start(f32[8]{0:T(128)} %gain_hbm.1) | copy-start | bytes 100

commit v9 on v8

--- a/solution.py
+++ b/solution.py
@@ -239,11 +239,19 @@
     def send_nodes(k, carry):
         row = lax.rem(m + k, n)
         nodes_copy(m, c, row, c).start()
-        nodes_copy(m, c, row, other).start()
+
+        @pl.when(is_last)
+        def _():
+            nodes_copy(m, c, row, other).start()
+
         return carry
 
     lax.fori_loop(1, n, send_nodes, 0)
-    nodes_copy(m, c, m, other).start()
+
+    @pl.when(is_last)
+    def _():
+        nodes_copy(m, c, m, other).start()
+
     send_load.wait()
 
     square = (own_blocks, own_blocks)
@@ -303,14 +311,23 @@
     pan_load.wait()
     running(pan_ref, pan_sum)
 
+    def wait_beside(row):
+        @pl.when(is_last)
+        def _():
+            nodes_copy(row, other, row, other).wait_send()
+
+        @pl.when(jnp.logical_not(is_last))
+        def _():
+            nodes_copy(row, other, row, other).wait_recv()
+
     def wait_nodes(k, carry):
         row = lax.rem(m + k, n)
         nodes_copy(row, c, row, c).wait()
-        nodes_copy(row, other, row, other).wait()
+        wait_beside(row)
         return carry
 
     lax.fori_loop(1, n, wait_nodes, 0)
-    nodes_copy(m, other, m, other).wait()
+    wait_beside(m)
 
     def cell_of(sums, tile, row, col):
         cell = tile * (KR * KC) + (row * KC + col)
@@ -512,11 +529,11 @@
     near_ms_send[...] = parts[0].astype(BF16)
     ms_hold[...] = parts[1]
     near_ms.start()
-    each(0, far // 2, pan_pair_to_twin)
     ms_own_parts(far)
     ms_z_send[far] = ms_total[0].astype(BF16)
     ms_z(far, near_row, pair).start()
     ms_mine[...] = ms_total[1]
+    each(0, far // 2, pan_pair_to_twin)
     each(0, far // 2, ms_far_onward)
     near_ms.wait_recv()
     ms_y_send[last] = (ms_hold[...] + near_ms_recv[...].astype(F32)).astype(BF16)

time: 32.7 us -> 31.8 us (0.972)
  Pallas kernels: 29.7 us -> 29 us
    pallas_call x1, Pallas kernels: 29.7 us -> 29 us  [local(): pl.pallas_call(functools.partial(mapping, capacity, col_grid.shape[1]), o...]
where the time goes in v9:
time: 31.8 us; the launch traced here: 31.7 us
  Pallas kernels  29 us (91%)
  other arithmetic  2.61 us (8%)
    pallas_call x1, Pallas kernels, local(): pl.pallas_call(functools.partial(mapping, capacity, col_grid.shape[1]), o...  29 us
    convert_element_type x1, other arithmetic, local(): return (mixed.astype(F32) + detail).astype(BF16)  2.61 us

profile of v9, /device:TPU:0, one launch (start us, length us, event | category | flops | bytes accessed | tf_op | source)
XLA Modules:
  0.0 31.7 jit_solution(1085752814241248628)
XLA Ops:
  0.0 0.0 copy-start
  0.0 29.0 %mapping.1 = (bf16[8,128,512]{2,1,0:T(8,128)(2,1)}, f32[128,512]{1,0:T(8,128)}) custom-call(s32[3,64]{1,0:T(4,128)} %send_hbm.1, f32[1,3]{1,0:T(1,128)} %bitcast.1, f32[1,8]{1,0:T(1,128)} %col_hbm.1, bf16[64,128,128]{2,1,0:T(8,128)(2,1)} %pan_hbm.1, bf16[64,32,256]{2,1,0:T(8,128)(2,1)} %ms_hbm.1, f32[8,8]{1,0:T(8,128)} %mix_hbm.1, f32[8]{0:T(128)} %gain_hbm.1, ...), custom_call_target="tpu_custom_call" | custom-call | tf_op jit(solution)/shard_map/mapping/pallas_call | solution.py:767
  29.0 0.0 copy-done
  29.0 2.6 %add_convert_fusion = bf16[8,128,512]{2,1,0:T(8,128)(2,1)} fusion(bf16[8,128,512]{2,1,0:T(8,128)(2,1)} %get-tuple-element.7, f32[128,512]{1,0:T(8,128)} %get-tuple-element.8, f32[8]{0:T(128)S(1)} %copy-done), kind=kLoop, calls=%fused_computation | loop fusion | flops 2097152 | bytes 2359328 | tf_op jit(solution)/shard_map/convert_element_type | solution.py:847
Async XLA Ops:
  0.0 29.0 %copy-start = (f32[8]{0:T(128)S(1)}, f32[8]{0:T(128)}, u32[]{:S(2)}) copy-start(f32[8]{0:T(128)} %gain_hbm.1) | copy-start | bytes 100

commit v10 on v9

--- a/solution.py
+++ b/solution.py
@@ -238,11 +238,12 @@
 
     def send_nodes(k, carry):
         row = lax.rem(m + k, n)
-        nodes_copy(m, c, row, c).start()
 
         @pl.when(is_last)
         def _():
             nodes_copy(m, c, row, other).start()
+
+        nodes_copy(m, c, row, c).start()
 
         return carry
 

time: 31.8 us -> 31.7 us (level)
  no operation moved by 1% of the time
where the time goes in v10:
time: 31.7 us; the launch traced here: 31.6 us
  Pallas kernels  29 us (91%)
  other arithmetic  2.61 us (8%)
    pallas_call x1, Pallas kernels, local(): pl.pallas_call(functools.partial(mapping, capacity, col_grid.shape[1]), o...  29 us
    convert_element_type x1, other arithmetic, local(): return (mixed.astype(F32) + detail).astype(BF16)  2.61 us

profile of v10, /device:TPU:0, one launch (start us, length us, event | category | flops | bytes accessed | tf_op | source)
XLA Modules:
  0.0 31.6 jit_solution(13354738760873803611)
XLA Ops:
  0.0 0.0 copy-start
  0.0 29.0 %mapping.1 = (bf16[8,128,512]{2,1,0:T(8,128)(2,1)}, f32[128,512]{1,0:T(8,128)}) custom-call(s32[3,64]{1,0:T(4,128)} %send_hbm.1, f32[1,3]{1,0:T(1,128)} %bitcast.1, f32[1,8]{1,0:T(1,128)} %col_hbm.1, bf16[64,128,128]{2,1,0:T(8,128)(2,1)} %pan_hbm.1, bf16[64,32,256]{2,1,0:T(8,128)(2,1)} %ms_hbm.1, f32[8,8]{1,0:T(8,128)} %mix_hbm.1, f32[8]{0:T(128)} %gain_hbm.1, ...), custom_call_target="tpu_custom_call" | custom-call | tf_op jit(solution)/shard_map/mapping/pallas_call | solution.py:768
  29.0 0.0 copy-done
  29.0 2.6 %add_convert_fusion = bf16[8,128,512]{2,1,0:T(8,128)(2,1)} fusion(bf16[8,128,512]{2,1,0:T(8,128)(2,1)} %get-tuple-element.7, f32[128,512]{1,0:T(8,128)} %get-tuple-element.8, f32[8]{0:T(128)S(1)} %copy-done), kind=kLoop, calls=%fused_computation | loop fusion | flops 2097152 | bytes 2359328 | tf_op jit(solution)/shard_map/convert_element_type | solution.py:848
Async XLA Ops:
  0.0 29.0 %copy-start = (f32[8]{0:T(128)S(1)}, f32[8]{0:T(128)}, u32[]{:S(2)}) copy-start(f32[8]{0:T(128)} %gain_hbm.1) | copy-start | bytes 100
